TPU v7x, 32 devices: a whole 2x2x4 slice. The times are simulated.
32 devices in a mesh: layer: 8 (over y, x, core), lat: 4 (over z).
Axes of the slice: x: 2, y: 2, z: 4, core: 2. Of those that a mesh axis runs over, the one named last changes fastest.
Arguments:
- activations: bfloat16 [1536, 4096], P('layer', 'lat'), may hold values from -6 to 6
- w_enc: bfloat16 [1536, 8192], P('layer', 'lat'), may hold values from -0.15625 to 0.15625
- w_dec: bfloat16 [1536, 8192], P('layer', 'lat'), may hold values from -0.25 to 0.25
- b_enc: bfloat16 [8192], P('lat'), may hold values from -3 to 3
- b_dec: float32 [1536], P('layer'), may hold values from -3 to 3
- tile_ids: int32 [4, 4], replicated, may hold values from -1 to 63, as said below
Outputs:
- d_w_enc: bfloat16 [1536, 8192], P('layer', 'lat')
- d_w_dec: bfloat16 [1536, 8192], P('layer', 'lat')
- d_b_enc: float32 [8192], P('lat')
Inputs may be any that keep to these rules, and one draw needn't show every extreme that they name: `tile_ids`: row b lists the tiles of block b: live ids first, then -1. Live ids of a row are distinct, and no two of them share an owner id // 16. Each row has at least half of 4 (rounded up) live slots; some row has 4. One owner is named in every row.
All inputs are finite; a program needn't handle non-finite values.
Results may differ from a plain program's by a relative error of at most 0.02.
The roundings to bfloat16 on the way count: a program that leaves them out, or rounds other values in their place, can miss the bound.
Values may be sent and summed in bfloat16 or wider, within the bound.
No kernel may reach another device: no remote copies, remote signals or barrier semaphores. Data moves between devices by JAX's collectives and lax.ppermute only.
A program may use at most 64 MiB of HBM per device.

v0:
```python
import math

import jax
import jax.numpy as jnp
from jax import lax
from jax.sharding import PartitionSpec as P

TILE = 128


def rounded(value):
    return lax.optimization_barrier(value.astype(jnp.bfloat16)).astype(jnp.float32)


def local(activations, w_enc, w_dec, b_enc, b_dec, tile_ids):
    feature_count, row_count = activations.shape
    latent_count = w_enc.shape[1]
    owner_count = lax.axis_size("lat")
    tile_count = latent_count // TILE
    position = lax.axis_index("lat")
    owner_ids = jnp.where(tile_ids >= 0, tile_ids // tile_count, -1)
    matched = owner_ids == position
    local_tile = jnp.sum(jnp.where(matched, tile_ids % tile_count, 0), axis=1)
    wanted = jnp.any(matched, axis=1)
    chosen = (local_tile[:, None] == jnp.arange(tile_count)[None, :]) & wanted[:, None]
    chosen_half = chosen.astype(jnp.bfloat16)
    enc_table = w_enc.reshape(feature_count, tile_count, TILE)
    dec_table = w_dec.reshape(feature_count, tile_count, TILE)
    bias_table = b_enc.reshape(tile_count, TILE)
    enc_send = jnp.einsum(
        "rt,ftc->rfc", chosen_half, enc_table, preferred_element_type=jnp.float32
    ).astype(jnp.bfloat16)
    dec_send = jnp.einsum(
        "rt,ftc->rfc", chosen_half, dec_table, preferred_element_type=jnp.float32
    ).astype(jnp.bfloat16)
    bias_send = jnp.dot(chosen_half, bias_table, preferred_element_type=jnp.float32).astype(
        jnp.bfloat16
    )
    enc_recv, dec_recv, bias_recv = (
        lax.all_to_all(enc_send, "lat", split_axis=0, concat_axis=0, tiled=True),
        lax.all_to_all(dec_send, "lat", split_axis=0, concat_axis=0, tiled=True),
        lax.all_to_all(bias_send, "lat", split_axis=0, concat_axis=0, tiled=True),
    )
    my_list = lax.dynamic_index_in_dim(tile_ids, position, 0, keepdims=False)
    live_slot = my_list >= 0
    source = jnp.where(live_slot, my_list // tile_count, 0)
    live_half = live_slot.astype(jnp.bfloat16)
    live_float = live_slot.astype(jnp.float32)
    enc_cols = jnp.take(enc_recv, source, axis=0) * live_half[:, None, None]
    bias_cols = jnp.take(bias_recv, source, axis=0).astype(jnp.float32)
    partial_value = rounded(
        jnp.einsum("fr,kfc->rkc", activations, enc_cols, preferred_element_type=jnp.float32)
    )
    preact = lax.psum(partial_value, "layer") + bias_cols[None]
    latent_codes = (jax.nn.relu(preact) * live_float[None, :, None]).astype(jnp.bfloat16)
    dec_cols = jnp.take(dec_recv, source, axis=0) * live_half[:, None, None]
    rebuilt = (
        jnp.einsum("rkc,kfc->fr", latent_codes, dec_cols, preferred_element_type=jnp.float32)
        + b_dec[:, None]
    )
    residual = rebuilt - activations.astype(jnp.float32)
    grad_err = (residual / math.sqrt(row_count)).astype(jnp.bfloat16)
    dec_grad = jnp.einsum(
        "fr,rkc->kfc", grad_err, latent_codes, preferred_element_type=jnp.float32
    ).astype(jnp.bfloat16)
    back_part = rounded(
        jnp.einsum("fr,kfc->rkc", grad_err, dec_cols, preferred_element_type=jnp.float32)
    )
    grad_total = lax.psum(back_part, "layer")
    code_grad = (grad_total * (latent_codes > 0)).astype(jnp.bfloat16)
    enc_grad = jnp.einsum(
        "fr,rkc->kfc", activations, code_grad, preferred_element_type=jnp.float32
    ).astype(jnp.bfloat16)
    bias_grad = jnp.sum(code_grad, axis=0, dtype=jnp.float32).astype(jnp.bfloat16)
    placement = ((source[:, None] == jnp.arange(owner_count)[None, :]) & live_slot[:, None]).astype(
        jnp.bfloat16
    )
    enc_return = jnp.einsum(
        "ko,kfc->ofc", placement, enc_grad, preferred_element_type=jnp.float32
    ).astype(jnp.bfloat16)
    dec_return = jnp.einsum(
        "ko,kfc->ofc", placement, dec_grad, preferred_element_type=jnp.float32
    ).astype(jnp.bfloat16)
    bias_return = jnp.einsum(
        "ko,kc->oc", placement, bias_grad, preferred_element_type=jnp.float32
    ).astype(jnp.bfloat16)
    enc_got, dec_got, bias_got = (
        lax.all_to_all(enc_return, "lat", split_axis=0, concat_axis=0, tiled=True),
        lax.all_to_all(dec_return, "lat", split_axis=0, concat_axis=0, tiled=True),
        lax.all_to_all(bias_return, "lat", split_axis=0, concat_axis=0, tiled=True),
    )
    d_w_enc = (
        jnp.einsum("rt,rfc->ftc", chosen_half, enc_got, preferred_element_type=jnp.float32)
        .reshape(feature_count, latent_count)
        .astype(jnp.bfloat16)
    )
    d_w_dec = (
        jnp.einsum("rt,rfc->ftc", chosen_half, dec_got, preferred_element_type=jnp.float32)
        .reshape(feature_count, latent_count)
        .astype(jnp.bfloat16)
    )
    d_b_enc = jnp.einsum(
        "rt,rc->tc", chosen_half, bias_got, preferred_element_type=jnp.float32
    ).reshape(latent_count)
    return (d_w_enc, d_w_dec, d_b_enc)


def solution(mesh):
    return jax.shard_map(
        local,
        mesh=mesh,
        in_specs=(
            P("layer", "lat"),
            P("layer", "lat"),
            P("layer", "lat"),
            P("lat"),
            P("layer"),
            P(),
        ),
        out_specs=(P("layer", "lat"), P("layer", "lat"), P("lat")),
        check_vma=False,
    )
```

profile of v0, /device:TPU:0, one launch (start us, length us, event | category | flops | bytes accessed | tf_op | source)
XLA Modules:
  0.0 188.2 jit_solution(17841347270297134224)
XLA Ops:
  7.2 0.9 fusion.44
  8.1 0.8 fusion.23
  9.7 6.3 %all-to-all-start.1 = ((bf16[4,1,128]{2,1,0:T(2,128)(2,1)}), bf16[4,1,128]{2,1,0:T(2,128)(2,1)S(1)}, u32[]{:S(2)}, u32[]{:S(2)}) async-start(bf16[4,1,128]{2,1,0:T(2,128)(2,1)} %copy.46), calls=%async_computation.1 | async-start | bytes 4096 | tf_op jit(solution)/shard_map/all_to_all | solution.py:42
  16.7 0.7 compare_and_fusion
  17.5 1.3 copy.65
  21.6 5.1 %all-to-all-start = ((bf16[4,192,128]{2,1,0:T(8,128)(2,1)}), bf16[4,192,128]{2,1,0:T(8,128)(2,1)S(1)}, u32[]{:S(2)}, u32[]{:S(2)}) async-start(bf16[4,192,128]{2,1,0:T(8,128)(2,1)} %copy.45), calls=%async_computation | async-start | bytes 393216 | tf_op jit(solution)/shard_map/all_to_all | solution.py:40
  27.3 6.6 %all-to-all-done = bf16[4,192,128]{2,1,0:T(8,128)(2,1)S(1)} async-done(((bf16[4,192,128]{2,1,0:T(8,128)(2,1)}), bf16[4,192,128]{2,1,0:T(8,128)(2,1)S(1)}, u32[]{:S(2)}, u32[]{:S(2)}) %all-to-all-start) | async-done | bytes 196640 | tf_op jit(solution)/shard_map/all_to_all | solution.py:40
  34.0 3.4 %all-to-all-start.2 = ((bf16[4,192,128]{2,1,0:T(8,128)(2,1)}), bf16[4,192,128]{2,1,0:T(8,128)(2,1)S(1)}, u32[]{:S(2)}, u32[]{:S(2)}) async-start(bf16[4,192,128]{2,1,0:T(8,128)(2,1)} %copy.47), calls=%async_computation.2 | async-start | bytes 393216 | tf_op jit(solution)/shard_map/all_to_all | solution.py:41
  38.6 56.5 %all-reduce.4 = f32[1024,4,128]{0,2,1:T(8,128)S(1)} all-reduce(bf16[1024,4,128]{0,2,1:T(8,128)(2,1)S(1)} %fusion), channel_id=1, replica_groups=mesh['layer'=8,'lat'=4] {'layer'}, use_global_device_ids=true, to_apply=%region_2.4 | all-reduce | flops 524288 | bytes 3145728 | tf_op jit(solution)/shard_map/psum | solution.py:54
  95.4 1.2 gather_fusion.2
  96.7 1.6 fusion.5
  98.3 1.6 convolution_convert_fusion
  100.4 1.0 convolution_convert_fusion.8
  102.1 5.0 %all-to-all-start.4 = ((bf16[4,192,128]{2,1,0:T(8,128)(2,1)}), bf16[4,192,128]{2,1,0:T(8,128)(2,1)S(1)}, u32[]{:S(2)}, u32[]{:S(2)}) async-start(bf16[4,192,128]{2,1,0:T(8,128)(2,1)} %copy.56), calls=%async_computation.4 | async-start | bytes 393216 | tf_op jit(solution)/shard_map/all_to_all | solution.py:89
  107.1 49.9 %all-reduce.3.cloned.1.call-done = bf16[1024,4,128]{0,2,1:T(8,128)(2,1)} async-done(((bf16[1024,4,128]{0,2,1:T(8,128)(2,1)}), bf16[1024,4,128]{0,2,1:T(8,128)(2,1)}) %all-reduce.3.cloned.1.call-update) | async-done | bytes 1048592 | tf_op jit(solution)/shard_map/psum | solution.py:69
  157.0 2.0 %fusion.41 = bf16[4,128]{1,0:T(4,128)(2,1)S(1)} fusion(bf16[1024,4,128]{0,2,1:T(8,128)(2,1)} %all-reduce.3.cloned.1.call-done, f32[4]{0:T(128)S(1)} %copy-done.9, f32[1024,4,128]{0,2,1:T(8,128)S(1)} %all-reduce.4, f32[4,128]{1,0:T(4,128)S(1)} %select_convert_fusion.1), kind=kLoop, calls=%fused_computation.90 | loop fusion | flops 4718080 | bytes 3148816 | tf_op jit(solution)/shard_map/reduce_sum | solution.py:74
  160.2 4.5 %all-to-all-start.5 = ((bf16[4,1,128]{2,1,0:T(2,128)(2,1)}), bf16[4,1,128]{2,1,0:T(2,128)(2,1)S(1)}, u32[]{:S(2)}, u32[]{:S(2)}) async-start(bf16[4,1,128]{2,1,0:T(2,128)(2,1)} %copy.58), calls=%async_computation.5 | async-start | bytes 4096 | tf_op jit(solution)/shard_map/all_to_all | solution.py:90
  165.0 0.7 copy.52
  165.7 4.5 %all-to-all-done.5 = bf16[4,1,128]{2,1,0:T(2,128)(2,1)S(1)} async-done(((bf16[4,1,128]{2,1,0:T(2,128)(2,1)}), bf16[4,1,128]{2,1,0:T(2,128)(2,1)S(1)}, u32[]{:S(2)}, u32[]{:S(2)}) %all-to-all-start.5) | async-done | bytes 1056 | tf_op jit(solution)/shard_map/all_to_all | solution.py:90
  170.2 3.4 %all-to-all-start.3 = ((bf16[4,192,128]{2,1,0:T(8,128)(2,1)}), bf16[4,192,128]{2,1,0:T(8,128)(2,1)S(1)}, u32[]{:S(2)}, u32[]{:S(2)}) async-start(bf16[4,192,128]{2,1,0:T(8,128)(2,1)} %copy.52), calls=%async_computation.3 | async-start | bytes 393216 | tf_op jit(solution)/shard_map/all_to_all | solution.py:88
  174.0 1.1 copy.84
  175.1 0.8 convolution_bitcast_fusion.1
  175.9 3.9 %all-to-all-done.3 = bf16[4,192,128]{2,1,0:T(8,128)(2,1)S(1)} async-done(((bf16[4,192,128]{2,1,0:T(8,128)(2,1)}), bf16[4,192,128]{2,1,0:T(8,128)(2,1)S(1)}, u32[]{:S(2)}, u32[]{:S(2)}) %all-to-all-start.3) | async-done | bytes 196640 | tf_op jit(solution)/shard_map/all_to_all | solution.py:88
  180.2 1.1 copy.85
  (60 shorter events, 10.0 us)
Async XLA Ops:
  7.2 1.8 copy-start
  7.2 11.8 %copy-start.2 = (bf16[192,2048]{1,0:T(8,128)(2,1)S(1)}, bf16[192,2048]{1,0:T(8,128)(2,1)}, u32[]{:S(2)}) copy-start(bf16[192,2048]{1,0:T(8,128)(2,1)} %param.10) | copy-start | bytes 2359300
  9.7 11.9 %all-to-all-start.1 = ((bf16[4,1,128]{2,1,0:T(2,128)(2,1)}), bf16[4,1,128]{2,1,0:T(2,128)(2,1)S(1)}, u32[]{:S(2)}, u32[]{:S(2)}) async-start(bf16[4,1,128]{2,1,0:T(2,128)(2,1)} %copy.46), calls=%async_computation.1 | async-start | bytes 4096 | tf_op jit(solution)/shard_map/all_to_all | solution.py:42
  16.7 2.8 %copy-start.10 = (pred[4]{0:T(512)(128)(4,1)}, pred[4]{0:T(512)(128)(4,1)S(1)}, u32[]{:S(2)}) copy-start(pred[4]{0:T(512)(128)(4,1)S(1)} %get-tuple-element.5) | copy-start | bytes 16
  16.7 78.4 %copy-start.8 = (f32[4]{0:T(128)}, f32[4]{0:T(128)S(1)}, u32[]{:S(2)}) copy-start(f32[4]{0:T(128)S(1)} %get-tuple-element.4) | copy-start | bytes 52
  17.4 1.8 copy-start.12
  17.4 78.0 %copy-start.6 = (bf16[4]{0:T(256)(128)(2,1)}, bf16[4]{0:T(256)(128)(2,1)S(1)}, u32[]{:S(2)}) copy-start(bf16[4]{0:T(256)(128)(2,1)S(1)} %get-tuple-element.10) | copy-start | bytes 28
  19.0 19.0 %copy-start.4 = (bf16[192,1024]{1,0:T(8,128)(2,1)S(1)}, bf16[192,1024]{1,0:T(8,128)(2,1)}, u32[]{:S(2)}) copy-start(bf16[192,1024]{1,0:T(8,128)(2,1)} %param.8) | copy-start | bytes 1179652
  21.6 12.4 %all-to-all-start = ((bf16[4,192,128]{2,1,0:T(8,128)(2,1)}), bf16[4,192,128]{2,1,0:T(8,128)(2,1)S(1)}, u32[]{:S(2)}, u32[]{:S(2)}) async-start(bf16[4,192,128]{2,1,0:T(8,128)(2,1)} %copy.45), calls=%async_computation | async-start | bytes 393216 | tf_op jit(solution)/shard_map/all_to_all | solution.py:40
  34.0 61.4 %all-to-all-start.2 = ((bf16[4,192,128]{2,1,0:T(8,128)(2,1)}), bf16[4,192,128]{2,1,0:T(8,128)(2,1)S(1)}, u32[]{:S(2)}, u32[]{:S(2)}) async-start(bf16[4,192,128]{2,1,0:T(8,128)(2,1)} %copy.47), calls=%async_computation.2 | async-start | bytes 393216 | tf_op jit(solution)/shard_map/all_to_all | solution.py:41
  37.3 119.6 %all-reduce.3.cloned.1.call-start = ((), (), s32[]{:S(2)}) async-start(), calls=%async_computation.6 | async-start | bytes 2097152 | tf_op jit(solution)/shard_map/psum | solution.py:69
  96.7 1.6 copy-start.3
  96.7 1.6 copy-start.7
  99.9 57.1 %copy-start.9 = (f32[4]{0:T(128)S(1)}, f32[4]{0:T(128)}, u32[]{:S(2)}) copy-start(f32[4]{0:T(128)} %copy-done.8) | copy-start | bytes 52
  100.4 58.5 %copy-start.11 = (pred[4]{0:T(512)(128)(4,1)S(1)}, pred[4]{0:T(512)(128)(4,1)}, u32[]{:S(2)}) copy-start(pred[4]{0:T(512)(128)(4,1)} %copy-done.10) | copy-start | bytes 16
  100.4 58.5 %copy-start.13 = (s32[4]{0:T(128)S(1)}, s32[4]{0:T(128)}, u32[]{:S(2)}) copy-start(s32[4]{0:T(128)} %copy-done.12) | copy-start | bytes 52
  102.1 58.1 %all-to-all-start.4 = ((bf16[4,192,128]{2,1,0:T(8,128)(2,1)}), bf16[4,192,128]{2,1,0:T(8,128)(2,1)S(1)}, u32[]{:S(2)}, u32[]{:S(2)}) async-start(bf16[4,192,128]{2,1,0:T(8,128)(2,1)} %copy.56), calls=%async_computation.4 | async-start | bytes 393216 | tf_op jit(solution)/shard_map/all_to_all | solution.py:89
  156.9 2.7 %copy-start.1 = (bf16[1024,4,128]{0,2,1:T(8,128)(2,1)S(1)}, bf16[1024,4,128]{0,2,1:T(8,128)(2,1)}, u32[]{:S(2)}) copy-start(bf16[1024,4,128]{0,2,1:T(8,128)(2,1)} %all-reduce.3.cloned.1.call-done) | copy-start | bytes 3145732
  156.9 2.7 %copy-start.5 = (bf16[192,1024]{1,0:T(8,128)(2,1)S(1)}, bf16[192,1024]{1,0:T(8,128)(2,1)}, u32[]{:S(2)}) copy-start(bf16[192,1024]{1,0:T(8,128)(2,1)} %param.8) | copy-start | bytes 1179652
  160.2 10.0 %all-to-all-start.5 = ((bf16[4,1,128]{2,1,0:T(2,128)(2,1)}), bf16[4,1,128]{2,1,0:T(2,128)(2,1)S(1)}, u32[]{:S(2)}, u32[]{:S(2)}) async-start(bf16[4,1,128]{2,1,0:T(2,128)(2,1)} %copy.58), calls=%async_computation.5 | async-start | bytes 4096 | tf_op jit(solution)/shard_map/all_to_all | solution.py:90
  170.2 9.6 %all-to-all-start.3 = ((bf16[4,192,128]{2,1,0:T(8,128)(2,1)}), bf16[4,192,128]{2,1,0:T(8,128)(2,1)S(1)}, u32[]{:S(2)}, u32[]{:S(2)}) async-start(bf16[4,192,128]{2,1,0:T(8,128)(2,1)} %copy.52), calls=%async_computation.3 | async-start | bytes 393216 | tf_op jit(solution)/shard_map/all_to_all | solution.py:88
Sparse Core Ops, SparseCore 0:
  100.0 56.8 all-reduce.2
where the time goes:
time: 189 us; the launch traced here: 188 us
  waiting for transfers between devices  65 us (34%)
  blocking collectives  56.5 us (30%)
  starting transfers between devices  27.7 us (15%)
  between operations  14.3 us (8%)
  local copies, waits for them, and re-layouts  10.1 us (5%)
  matrix products  8.36 us (4%)
  other arithmetic  6.22 us (3%)
    psum x1, blocking collectives, local(): preact = lax.psum(partial_value, 'layer') + bias_cols[None]  56.5 us
    psum x1, waiting for transfers between devices, local(): grad_total = lax.psum(back_part, 'layer')  49.9 us
    all_to_all x1, waiting for transfers between devices, local(): lax.all_to_all(enc_send, 'lat', split_axis=0, concat_axis=0, tiled=True)  6.63 us
    all_to_all x1, starting transfers between devices, local(): lax.all_to_all(bias_send, 'lat', split_axis=0, concat_axis=0, tiled=True)  6.35 us
    all_to_all x1, starting transfers between devices, local(): lax.all_to_all(enc_send, 'lat', split_axis=0, concat_axis=0, tiled=True)  5.09 us
    all_to_all x1, starting transfers between devices, local(): lax.all_to_all(dec_return, 'lat', split_axis=0, concat_axis=0, tiled=True)  4.97 us
    all_to_all x1, starting transfers between devices, local(): lax.all_to_all(bias_return, 'lat', split_axis=0, concat_axis=0, tiled=True)  4.55 us
    all_to_all x1, waiting for transfers between devices, local(): lax.all_to_all(bias_return, 'lat', split_axis=0, concat_axis=0, tiled=True)  4.53 us
  transfers between devices with their start and end apart: 7, of which 4 were waited for; matrix products, arithmetic and copies ran while one was open for 9% of the time, Pallas kernels for 0%

commit v1 on v0

v1 whole, which is shorter than its diff:
```python
import functools
import math

import jax
import jax.numpy as jnp
from jax import lax
from jax.experimental import pallas as pl
from jax.experimental.pallas import tpu as pltpu
from jax.sharding import PartitionSpec as P

TILE = 128
PARTS = 4
EXTRA = 16
F32 = jnp.float32
BF16 = jnp.bfloat16


def vmem():
    return pl.BlockSpec(memory_space=pltpu.VMEM)


def smem():
    return pl.BlockSpec(memory_space=pltpu.SMEM)


def anywhere():
    return pl.BlockSpec(memory_space=pl.ANY)


def dot(a, b, da, db):
    return lax.dot_general(a, b, (((da,), (db,)), ((), ())), preferred_element_type=F32)


def call(kernel, outs, ins, args, out_specs=None, scratch=(), limit=8 << 20, alias=None):
    return pl.pallas_call(
        kernel,
        out_shape=outs,
        in_specs=ins,
        out_specs=jax.tree.map(lambda _: vmem(), outs) if out_specs is None else out_specs,
        scratch_shapes=list(scratch),
        input_output_aliases=alias or {},
        compiler_params=pltpu.CompilerParams(vmem_limit_bytes=limit),
        cost_estimate=pl.CostEstimate(flops=10**8, bytes_accessed=10**6, transcendentals=0),
    )(*args)


def shape(*dims, kind=BF16):
    return jax.ShapeDtypeStruct(dims, kind)


def place(parts):
    layer = lax.axis_index("layer")
    cores = lax.axis_size("layer") // parts
    return lax.axis_index("lat"), lax.div(layer, cores), lax.rem(layer, cores)


def xor(a, b):
    return jnp.bitwise_xor(a, b)


def lanes(index, size):
    return pl.ds(pl.multiple_of(index * size, size), size)


def wanted_tile(ids_ref, block, owner, tiles):
    found = jnp.int32(-1)
    base = owner * tiles
    for slot in range(ids_ref.shape[1]):
        tile = ids_ref[block, slot]
        here = (tile >= base) & (tile < base + tiles)
        found = jnp.where(here, tile - base, found)
    return found


def send_lanes(ids_ref, me, step, tiles):
    tile = wanted_tile(ids_ref, xor(me, step), me, tiles)
    return lanes(jnp.maximum(tile, 0), TILE)


def first_kernel(owners, tiles, parts, ids_ref, enc_ref, dec_ref, bias_ref, *rest):
    outs, sem = rest[:-1], rest[-1]
    features = enc_ref.shape[0]
    me, _, _ = place(parts)
    copies = []
    for step in range(1, owners):
        where = send_lanes(ids_ref, me, step, tiles)
        for index, source in enumerate((enc_ref, dec_ref)):
            target = outs[step - 1].at[pl.ds(index * features, features), :]
            copies.append(pltpu.make_async_copy(source.at[:, where], target, sem.at[len(copies)]))
    for copy in copies:
        copy.start()
    for step in range(1, owners):
        bias = bias_ref[:, send_lanes(ids_ref, me, step, tiles)]
        outs[step - 1][pl.ds(2 * features, EXTRA), :] = jnp.broadcast_to(bias, (EXTRA, TILE))
    for copy in copies:
        copy.wait()


def second_kernel(tiles, parts, ids_ref, acts_ref, enc_ref, dec_ref, bias_ref, offset_ref, *rest):
    messages, bias_out, sem = rest[:parts], rest[-2], rest[-1]
    features, rows = acts_ref.shape
    quarter = rows // parts
    me, part, _ = place(parts)
    inner = pl.ds(0, features)
    here = send_lanes(ids_ref, me, 0, tiles)
    copies = []
    for step in range(parts):
        out = messages[step]
        acts = acts_ref.at[:, lanes(xor(part, step), quarter)]
        start = 0
        for source in (acts, enc_ref.at[:, here], dec_ref.at[:, here]):
            size = source.shape[1]
            target = out.at[inner, pl.ds(start, size)]
            copies.append(pltpu.make_async_copy(source, target, sem.at[len(copies)]))
            start += size
    for copy in copies:
        copy.start()
    offset = offset_ref[...]
    high = offset.astype(BF16)
    rest_one = offset - high.astype(F32)
    middle = rest_one.astype(BF16)
    low = (rest_one - middle.astype(F32)).astype(BF16)
    row = lax.broadcasted_iota(jnp.int32, (EXTRA, features), 0)
    split = jnp.where(row == 0, high.astype(F32), 0.0)
    split = jnp.where(row == 1, middle.astype(F32), split)
    split = jnp.where(row == 2, low.astype(F32), split).astype(BF16)
    for step in range(parts):
        messages[step][pl.ds(features, EXTRA), :] = jnp.zeros((EXTRA, quarter + 2 * TILE), BF16)
        messages[step][pl.ds(features, EXTRA), pl.ds(0, features)] = split
    bias_out[...] = jnp.broadcast_to(bias_ref[:, here], (EXTRA, TILE))
    for copy in copies:
        copy.wait()


def join_kernel(owners, bias_ref, *refs):
    got, enc_out, dec_out, bias_out = refs[: owners - 1], refs[-3], refs[-2], refs[-1]
    features = enc_out.shape[0]
    bias_out[:, pl.ds(0, TILE)] = bias_ref[...]
    for step in range(owners - 1):
        enc_out[:, pl.ds(step * TILE, TILE)] = got[step][pl.ds(0, features), :]
        dec_out[:, pl.ds(step * TILE, TILE)] = got[step][pl.ds(features, features), :]
        bias_out[:, pl.ds((step + 1) * TILE, TILE)] = got[step][pl.ds(2 * features, EXTRA), :]


def zero_kernel(*refs):
    outs, hold, sem = refs[:-2], refs[-2], refs[-1]
    hold[...] = jnp.zeros_like(hold)
    width = hold.shape[1]
    copies = []
    for out in outs:
        for start in range(0, out.shape[1], width):
            target = out.at[:, pl.ds(start, width)]
            copies.append(pltpu.make_async_copy(hold, target, sem.at[len(copies)]))
    for copy in copies:
        copy.start()
    for copy in copies:
        copy.wait()


def preact_kernel(parts, *refs):
    messages, encs, out_ref = refs[:parts], refs[parts : 2 * parts], refs[-1]
    features = encs[0].shape[0]
    quarter = out_ref.shape[1]
    inner = pl.ds(0, features)
    one, two = None, None
    for step in range(parts):
        acts = messages[step][inner, pl.ds(0, quarter)]
        first = dot(messages[step][inner, pl.ds(quarter, TILE)], acts, 0, 0).astype(BF16).astype(F32)
        second = dot(encs[step][...], acts, 0, 0).astype(BF16).astype(F32)
        one = first if one is None else one + first
        two = second if two is None else two + second
    out_ref[pl.ds(0, TILE), :] = one
    out_ref[pl.ds(TILE, out_ref.shape[0] - TILE), :] = two


def codes_kernel(owners, tiles, parts, ids_ref, mine_ref, other_ref, bias_ref, out_ref):
    me, _, _ = place(parts)
    quarter = out_ref.shape[1]
    row = lax.broadcasted_iota(jnp.int32, (EXTRA, quarter), 0)
    pick = jnp.where(row == 0, 1.0, 0.0).astype(BF16)
    for step in range(owners):
        live = wanted_tile(ids_ref, me, xor(me, step), tiles) >= 0
        where = pl.ds(step * TILE, TILE)
        bias = dot(bias_ref[:, where], pick, 0, 0)
        pre = mine_ref[where, :] + other_ref[where, :] + bias
        out_ref[where, :] = jnp.where(live, jnp.maximum(pre, 0.0), 0.0).astype(BF16)


def decode_kernel(count, cores, parts, scale, first, last, codes_ref, *refs):
    refs = list(refs)
    before = None if first else refs.pop(0)
    messages, decs = refs[:count], refs[count : 2 * count]
    grads = refs[2 * count : 3 * count]
    outs = refs[3 * count :]
    features, width = grads[0].shape
    quarter = codes_ref.shape[1]
    inner = pl.ds(0, features)
    row = lax.broadcasted_iota(jnp.int32, (EXTRA, quarter), 0)
    pick = jnp.where(row < 3, 1.0, 0.0).astype(BF16)
    codes = codes_ref[...]
    one = None if first else before[pl.ds(0, TILE), :]
    two = None if first else before[pl.ds(TILE, width - TILE), :]
    for step in range(count):
        message, dec = messages[step], decs[step][...]
        acts = message[inner, pl.ds(0, quarter)].astype(F32)
        tile = message[inner, pl.ds(quarter + TILE, TILE)]
        offset = dot(message[pl.ds(features, EXTRA), pl.ds(0, features)], pick, 0, 0)
        rebuilt = dot(tile, codes[:TILE], 1, 0) + dot(dec, codes[TILE:], 1, 0) + offset
        err = ((rebuilt - acts) * scale).astype(BF16)
        grads[step][...] = dot(err, codes, 1, 1).astype(BF16)
        left = dot(tile, err, 0, 0).astype(BF16).astype(F32)
        right = dot(dec, err, 0, 0).astype(BF16).astype(F32)
        one = left if one is None else one + left
        two = right if two is None else two + right
    total = outs[-1]
    total[pl.ds(0, TILE), :] = one
    total[pl.ds(TILE, width - TILE), :] = two
    if last:
        _, _, core = place(parts)
        half = width // cores
        for step in range(cores):
            outs[step][...] = total[lanes(xor(core, step), half), :]


def mask_kernel(parts, codes_ref, *refs):
    sums, out_ref = refs[:-1], refs[-1]
    _, _, core = place(parts)
    codes = codes_ref[lanes(core, out_ref.shape[0]), :].astype(F32)
    total = sums[0][...]
    for other in sums[1:]:
        total = total + other[...]
    out_ref[...] = jnp.where(codes > 0, total, 0.0).astype(BF16)


def sum_kernel(parts, owners, *refs):
    total = None
    for step in range(parts):
        part = refs[step][...].astype(F32)
        total = part if total is None else total + part
    total = total.astype(BF16)
    for step in range(owners):
        refs[parts + step][...] = total[:, step * TILE : (step + 1) * TILE]


def encgrad_kernel(parts, cores, owners, *refs):
    acts, pieces = refs[:cores], refs[cores : cores + parts]
    outs, all_ref = refs[cores + parts : -1], refs[-1]
    quarter = pieces[0].shape[1]
    features = acts[0].shape[0]
    share = owners // cores
    _, part, _ = place(parts)
    for step in range(parts):
        all_ref[:, lanes(xor(part, step), quarter)] = pieces[step][...]
    grads = all_ref[...]
    bias = dot(jnp.ones((EXTRA, grads.shape[1]), BF16), grads, 1, 1).astype(BF16)
    for step in range(cores):
        back = dot(acts[step][...], grads, 1, 1).astype(BF16)
        for tile in range(share):
            where = slice(tile * TILE, (tile + 1) * TILE)
            outs[step * share + tile][pl.ds(0, features), :] = back[:, where]
            outs[step * share + tile][pl.ds(features, EXTRA), :] = bias[:, where]


def place_kernel(owners, cores, tiles, parts, crossed, ids_ref, zero_ref, *refs):
    got, out_ref = refs[:owners], refs[owners]
    hold, sem = refs[-2], refs[-1]
    features = out_ref.shape[0]
    me, _, core = place(parts)
    share = owners // cores
    found = []
    for step in range(owners):
        slot = xor(core, step // share) * share + step % share if crossed else step
        found.append(wanted_tile(ids_ref, xor(me, slot), me, tiles))
    if crossed:
        refs[owners + 1][...] = jnp.zeros_like(refs[owners + 1])
    fresh = []
    for step in range(owners):
        new = found[step] >= 0
        for peer in range(step):
            new = new & (found[peer] != found[step])
        fresh.append(new)

    def copy(step):
        where = lanes(jnp.maximum(found[step], 0), TILE)
        return pltpu.make_async_copy(hold.at[step], out_ref.at[:, where], sem.at[step])

    for step in range(owners):

        @pl.when(fresh[step])
        def _():
            total = got[step][...].astype(F32)
            for peer in range(step + 1, owners):
                total = total + jnp.where(
                    found[peer] == found[step], got[peer][...].astype(F32), 0.0
                )
            hold[step] = total[:features].astype(BF16)
            copy(step).start()
            if crossed:
                refs[owners + 1][:, lanes(found[step], TILE)] = total[features : features + 1]

    for step in range(owners):

        @pl.when(fresh[step])
        def _():
            copy(step).wait()


def sizes(mesh):
    owners, layers = mesh.shape["lat"], mesh.shape["layer"]
    parts = min(PARTS, layers)
    return owners, layers, parts, layers // parts


def local(owners, layers, parts, cores, activations, w_enc, w_dec, b_enc, b_dec, tile_ids):
    features, rows = activations.shape
    latents = w_enc.shape[1]
    tiles = latents // TILE
    width = owners * TILE
    half = width // cores
    quarter = rows // parts
    share = owners // cores

    def over_lat(x, step):
        return lax.ppermute(x, "lat", [(i, i ^ step) for i in range(owners)])

    def over_layer(x, step, stride):
        return lax.ppermute(x, "layer", [(i, i ^ (step * stride)) for i in range(layers)])

    def crossed(x, step):
        pairs = []
        for layer in range(layers):
            part, core = layer // cores, layer % cores
            goal = part * cores + (core ^ (step // share))
            for z in range(owners):
                owner = z ^ (core * share + step % share)
                pairs.append((layer * owners + z, goal * owners + owner))
        return lax.ppermute(x, ("layer", "lat"), pairs)

    def gather(x):
        return [x] + [over_layer(x, s, cores) for s in range(1, parts)]

    bias_line = b_enc.reshape(1, latents)
    moved = call(
        functools.partial(first_kernel, owners, tiles, parts),
        [shape(2 * features + EXTRA, TILE)] * (owners - 1),
        [smem(), anywhere(), anywhere(), vmem()],
        (tile_ids, w_enc, w_dec, bias_line),
        scratch=[pltpu.SemaphoreType.DMA((2 * (owners - 1),))],
    )
    second = call(
        functools.partial(second_kernel, tiles, parts),
        [shape(features + EXTRA, quarter + 2 * TILE)] * parts + [shape(EXTRA, TILE)],
        [smem(), anywhere(), anywhere(), anywhere(), vmem(), vmem()],
        (tile_ids, activations, w_enc, w_dec, bias_line, b_dec.reshape(1, features)),
        scratch=[pltpu.SemaphoreType.DMA((3 * parts,))],
    )
    messages, own_bias = second[:parts], second[-1]
    moved = [over_lat(x, s + 1) for s, x in enumerate(moved)]
    messages = [messages[0]] + [over_layer(messages[s], s, cores) for s in range(1, parts)]
    all_acts = [activations] + [over_layer(activations, s, 1) for s in range(1, cores)]
    enc_rest, dec_rest, bias_rows = call(
        functools.partial(join_kernel, owners),
        [shape(features, width - TILE)] * 2 + [shape(EXTRA, width)],
        [vmem()] * owners,
        (own_bias, *moved),
    )
    encs = gather(enc_rest)
    decs = gather(dec_rest)

    mine = call(
        functools.partial(preact_kernel, parts),
        shape(width, quarter, kind=F32),
        [vmem()] * (2 * parts),
        (*messages, *encs),
    )
    step = 1
    while 2 * step < cores:
        mine = mine + over_layer(mine, step, 1)
        step = 2 * step
    other = over_layer(mine, step, 1)
    codes = call(
        functools.partial(codes_kernel, owners, tiles, parts),
        shape(width, quarter),
        [smem()] + [vmem()] * 3,
        (tile_ids, mine, other, bias_rows),
    )
    groups = [[0], list(range(1, parts - 1)), [parts - 1]]
    total, sent = None, []
    for index, group in enumerate(groups):
        first, last = index == 0, index == len(groups) - 1
        outs = [shape(features, width)] * len(group)
        if last:
            outs += [shape(half, quarter, kind=F32)] * cores
        outs += [shape(width, quarter, kind=F32)]
        args = [codes] + ([] if first else [total])
        args += [messages[s] for s in group] + [decs[s] for s in group]
        out = call(
            functools.partial(
                decode_kernel, len(group), cores, parts, 1.0 / math.sqrt(rows), first, last
            ),
            outs,
            [vmem()] * len(args),
            tuple(args),
        )
        sent += out[: len(group)]
        total = out[-1]
        sums = out[len(group) : -1]
    sums = [sums[0]] + [over_layer(sums[s], s, 1) for s in range(1, cores)]
    grad = call(
        functools.partial(mask_kernel, parts),
        shape(half, quarter),
        [vmem()] * (1 + cores),
        (codes, *sums),
    )
    grads = gather(grad)
    sent = [sent[0]] + [over_layer(sent[s], s, cores) for s in range(1, parts)]
    dec_back = call(
        functools.partial(sum_kernel, parts, owners),
        [shape(features, TILE)] * owners,
        [vmem()] * parts,
        tuple(sent),
    )
    dec_back = [dec_back[0]] + [over_lat(dec_back[s], s) for s in range(1, owners)]
    enc_back = call(
        functools.partial(encgrad_kernel, parts, cores, owners),
        [shape(features + EXTRA, TILE)] * owners,
        [vmem()] * (cores + parts),
        (*all_acts, *grads),
        scratch=[pltpu.VMEM((half, rows), BF16)],
    )
    enc_back = [crossed(x, s) for s, x in enumerate(enc_back)]
    zeros = call(
        zero_kernel,
        [shape(features, latents)] * 2,
        [],
        (),
        out_specs=[anywhere()] * 2,
        scratch=[
            pltpu.VMEM((features, 2 * TILE), BF16),
            pltpu.SemaphoreType.DMA((latents // TILE,)),
        ],
    )

    def put(cross, pieces, zero):
        outs = [shape(features, latents)] + ([shape(1, latents, kind=F32)] if cross else [])
        return call(
            functools.partial(place_kernel, owners, cores, tiles, parts, cross),
            outs,
            [smem(), anywhere()] + [vmem()] * owners,
            (tile_ids, zero, *pieces),
            out_specs=[anywhere()] + ([vmem()] if cross else []),
            scratch=[pltpu.VMEM((owners, features, TILE), BF16), pltpu.SemaphoreType.DMA((owners,))],
            alias={1: 0},
        )

    (d_w_dec,) = put(False, dec_back, zeros[0])
    d_w_enc, d_b_enc = put(True, enc_back, zeros[1])
    return (d_w_enc, d_w_dec, d_b_enc.reshape(latents))


def solution(mesh):
    owners, layers, parts, cores = sizes(mesh)

    def body(*args):
        return local(owners, layers, parts, cores, *args)

    return jax.shard_map(
        body,
        mesh=mesh,
        in_specs=(
            P("layer", "lat"),
            P("layer", "lat"),
            P("layer", "lat"),
            P("lat"),
            P("layer"),
            P(),
        ),
        out_specs=(P("layer", "lat"), P("layer", "lat"), P("lat")),
        check_vma=False,
    )
```

time: 189 us -> 75.2 us (0.40)
  blocking collectives: 56.5 us -> 0 us
  waiting for transfers between devices: 65 us -> 22.2 us
  between operations: 14.3 us -> 0.8 us
  Pallas kernels: 0 us -> 11.5 us
  matrix products: 8.36 us -> 0 us
  starting transfers between devices: 27.7 us -> 35.8 us
  other arithmetic: 6.22 us -> 0 us
  local copies, waits for them, and re-layouts: 10.1 us -> 4.65 us
    psum x1 -> x0, blocking collectives: 56.5 us -> none  [local(): preact = lax.psum(partial_value, 'layer') + bias_cols[None]]
    psum x1 -> x0, waiting for transfers between devices: 49.9 us -> none  [local(): grad_total = lax.psum(back_part, 'layer')]
    ppermute x0 -> x28, starting transfers between devices: none -> 35.8 us  [the longest x18 21.8 us: over_layer(): lax.ppermute(x, 'layer', [(i, i ^ step * stride) for i in range(layers)])]
    all_to_all x6 -> x0, starting transfers between devices: 27.7 us -> none  [the longest x1 6.35 us: local(): lax.all_to_all(bias_send, 'lat', split_axis=0, concat_axis=0, tiled=True)]
    ppermute x0 -> x28, waiting for transfers between devices: none -> 22.2 us  [the longest x18 15.9 us: over_layer(): lax.ppermute(x, 'layer', [(i, i ^ step * stride) for i in range(layers)])]
    all_to_all x6 -> x0, waiting for transfers between devices: 15.1 us -> none  [the longest x1 6.63 us: local(): lax.all_to_all(enc_send, 'lat', split_axis=0, concat_axis=0, tiled=True)]
    pallas_call x0 -> x14, Pallas kernels: none -> 11.5 us  [call(): pl.pallas_call(kernel, out_shape=outs, in_specs=ins, out_specs=jax.tree.m...]
    dot_general x14 -> x0, matrix products: 8.36 us -> none  [the longest x1 1.6 us: local(): jnp.einsum('fr,kfc->rkc', grad_err, dec_cols, preferred_element_type=jnp....]
  transfers between devices with their start and end apart: 7 -> 28, of which waited for: 4 -> 10; matrix products, arithmetic and copies ran while one was open for 9% -> 0% of each run, Pallas kernels for 0% -> 11%
where the time goes in v1:
time: 75.2 us; the launch traced here: 74.9 us
  starting transfers between devices  35.8 us (48%)
  waiting for transfers between devices  22.2 us (30%)
  Pallas kernels  11.5 us (15%)
  local copies, waits for them, and re-layouts  4.65 us (6%)
  between operations  0.8 us (1%)
    ppermute x18, starting transfers between devices, over_layer(): lax.ppermute(x, 'layer', [(i, i ^ step * stride) for i in range(layers)])  21.8 us
    ppermute x18, waiting for transfers between devices, over_layer(): lax.ppermute(x, 'layer', [(i, i ^ step * stride) for i in range(layers)])  15.9 us
    pallas_call x14, Pallas kernels, call(): pl.pallas_call(kernel, out_shape=outs, in_specs=ins, out_specs=jax.tree.m...  11.5 us
    ppermute x6, starting transfers between devices, over_lat(): return lax.ppermute(x, 'lat', [(i, i ^ step) for i in range(owners)])  9.38 us
    ppermute x6, waiting for transfers between devices, over_lat(): return lax.ppermute(x, 'lat', [(i, i ^ step) for i in range(owners)])  4.86 us
    ppermute x4, starting transfers between devices, crossed(): return lax.ppermute(x, ('layer', 'lat'), pairs)  4.61 us
    unnamed x16, local copies, waits for them, and re-layouts  3.95 us
  transfers between devices with their start and end apart: 28, of which 10 were waited for; matrix products, arithmetic and copies ran while one was open for 0% of the time, Pallas kernels for 11%

profile of v1, /device:TPU:0, one launch (start us, length us, event | category | flops | bytes accessed | tf_op | source)
XLA Modules:
  0.0 74.9 jit_solution(2515963154746074706)
XLA Ops:
  6.2 3.0 %collective-permute-start.1 = (bf16[208,512]{1,0:T(8,128)(2,1)S(1)}, bf16[208,512]{1,0:T(8,128)(2,1)S(1)}, u32[]{:S(2)}, u32[]{:S(2)}) collective-permute-start(bf16[208,512]{1,0:T(8,128)(2,1)S(1)} %get-tuple-element.36), channel_id=1, source_target_pairs={{0,8},{4,12},{8,0},{12,4},{16,24},{20,28},{24,16},{28,20},{1,9},{5... | collective-permute-start | bytes 638984 | tf_op jit(solution)/shard_map/ppermute | solution.py:327
  10.0 1.6 %collective-permute-start.4 = (bf16[400,128]{1,0:T(8,128)(2,1)S(1)}, bf16[400,128]{1,0:T(8,128)(2,1)S(1)}, u32[]{:S(2)}, u32[]{:S(2)}) collective-permute-start(bf16[400,128]{1,0:T(8,128)(2,1)S(1)} %get-tuple-element.40), channel_id=1, source_target_pairs={{0,1},{1,0},{2,3},{3,2},{4,5},{5,4},{6,7},{7,6},{8,9},{9,8},{10,11... | collective-permute-start | bytes 307208 | tf_op jit(solution)/shard_map/ppermute | solution.py:324
  11.7 2.6 %collective-permute-start.5 = (bf16[400,128]{1,0:T(8,128)(2,1)S(1)}, bf16[400,128]{1,0:T(8,128)(2,1)S(1)}, u32[]{:S(2)}, u32[]{:S(2)}) collective-permute-start(bf16[400,128]{1,0:T(8,128)(2,1)S(1)} %get-tuple-element.41), channel_id=1, source_target_pairs={{0,2},{1,3},{2,0},{3,1},{4,6},{5,7},{6,4},{7,5},{8,10},{9,11},{10,... | collective-permute-start | bytes 307208 | tf_op jit(solution)/shard_map/ppermute | solution.py:324
  14.5 1.5 %collective-permute-start.2 = (bf16[208,512]{1,0:T(8,128)(2,1)S(1)}, bf16[208,512]{1,0:T(8,128)(2,1)S(1)}, u32[]{:S(2)}, u32[]{:S(2)}) collective-permute-start(bf16[208,512]{1,0:T(8,128)(2,1)S(1)} %get-tuple-element.37), channel_id=1, source_target_pairs={{0,16},{4,20},{8,24},{12,28},{16,0},{20,4},{24,8},{28,12},{1,17},{... | collective-permute-start | bytes 638984 | tf_op jit(solution)/shard_map/ppermute | solution.py:327
  17.3 4.8 %collective-permute-done.5.refs_1_ = bf16[400,128]{1,0:T(8,128)(2,1)S(1)} collective-permute-done((bf16[400,128]{1,0:T(8,128)(2,1)S(1)}, bf16[400,128]{1,0:T(8,128)(2,1)S(1)}, u32[]{:S(2)}, u32[]{:S(2)}) %collective-permute-start.5) | collective-permute-done | bytes 102432 | tf_op jit(solution)/shard_map/ppermute | solution.py:324
  22.9 1.5 %collective-permute-start.8 = (bf16[192,384]{1,0:T(8,128)(2,1)S(1)}, bf16[192,384]{1,0:T(8,128)(2,1)S(1)}, u32[]{:S(2)}, u32[]{:S(2)}) collective-permute-start(bf16[192,384]{1,0:T(8,128)(2,1)S(1)} %get-tuple-element.43.refs_4_), channel_id=1, source_target_pairs={{0,16},{4,20},{8,24},{12,28},{16,0},{20,4},{24,8},{28,12},{1,17},{... | collective-permute-start | bytes 442376 | tf_op jit(solution)/shard_map/ppermute | solution.py:327
  24.4 1.3 %collective-permute-start.9 = (bf16[192,384]{1,0:T(8,128)(2,1)S(1)}, bf16[192,384]{1,0:T(8,128)(2,1)S(1)}, u32[]{:S(2)}, u32[]{:S(2)}) collective-permute-start(bf16[192,384]{1,0:T(8,128)(2,1)S(1)} %get-tuple-element.43.refs_4_), channel_id=1, source_target_pairs={{0,24},{4,28},{8,16},{12,20},{16,8},{20,12},{24,0},{28,4},{1,25},{... | collective-permute-start | bytes 442376 | tf_op jit(solution)/shard_map/ppermute | solution.py:327
  25.7 2.4 %collective-permute-done.2.refs_2_ = bf16[208,512]{1,0:T(8,128)(2,1)S(1)} collective-permute-done((bf16[208,512]{1,0:T(8,128)(2,1)S(1)}, bf16[208,512]{1,0:T(8,128)(2,1)S(1)}, u32[]{:S(2)}, u32[]{:S(2)}) %collective-permute-start.2) | collective-permute-done | bytes 213024 | tf_op jit(solution)/shard_map/ppermute | solution.py:327
  28.1 3.2 %collective-permute-done.8.refs_6_ = bf16[192,384]{1,0:T(8,128)(2,1)S(1)} collective-permute-done((bf16[192,384]{1,0:T(8,128)(2,1)S(1)}, bf16[192,384]{1,0:T(8,128)(2,1)S(1)}, u32[]{:S(2)}, u32[]{:S(2)}) %collective-permute-start.8) | collective-permute-done | bytes 147488 | tf_op jit(solution)/shard_map/ppermute | solution.py:327
  32.6 1.5 %collective-permute-start.12 = (bf16[192,384]{1,0:T(8,128)(2,1)S(1)}, bf16[192,384]{1,0:T(8,128)(2,1)S(1)}, u32[]{:S(2)}, u32[]{:S(2)}) collective-permute-start(bf16[192,384]{1,0:T(8,128)(2,1)S(1)} %get-tuple-element.45.refs_1_), channel_id=1, source_target_pairs={{0,16},{4,20},{8,24},{12,28},{16,0},{20,4},{24,8},{28,12},{1,17},{... | collective-permute-start | bytes 442376 | tf_op jit(solution)/shard_map/ppermute | solution.py:327
  34.1 1.3 %collective-permute-start.13 = (bf16[192,384]{1,0:T(8,128)(2,1)S(1)}, bf16[192,384]{1,0:T(8,128)(2,1)S(1)}, u32[]{:S(2)}, u32[]{:S(2)}) collective-permute-start(bf16[192,384]{1,0:T(8,128)(2,1)S(1)} %get-tuple-element.45.refs_1_), channel_id=1, source_target_pairs={{0,24},{4,28},{8,16},{12,20},{16,8},{20,12},{24,0},{28,4},{1,25},{... | collective-permute-start | bytes 442376 | tf_op jit(solution)/shard_map/ppermute | solution.py:327
  36.9 1.8 %collective-permute-done.11.refs_3_ = bf16[192,384]{1,0:T(8,128)(2,1)S(1)} collective-permute-done((bf16[192,384]{1,0:T(8,128)(2,1)S(1)}, bf16[192,384]{1,0:T(8,128)(2,1)S(1)}, u32[]{:S(2)}, u32[]{:S(2)}) %collective-permute-start.11) | collective-permute-done | bytes 147488 | tf_op jit(solution)/shard_map/ppermute | solution.py:327
  38.7 2.1 %collective-permute-done.12.refs_4_ = bf16[192,384]{1,0:T(8,128)(2,1)S(1)} collective-permute-done((bf16[192,384]{1,0:T(8,128)(2,1)S(1)}, bf16[192,384]{1,0:T(8,128)(2,1)S(1)}, u32[]{:S(2)}, u32[]{:S(2)}) %collective-permute-start.12) | collective-permute-done | bytes 147488 | tf_op jit(solution)/shard_map/ppermute | solution.py:327
  42.2 1.4 %shard_map.93 = (bf16[192,512]{1,0:T(8,128)(2,1)S(1)}, f32[256,256]{1,0:T(8,128)S(1)}, f32[256,256]{1,0:T(8,128)S(1)}, f32[512,256]{1,0:T(8,128)}) custom-call(bf16[512,256]{1,0:T(8,128)(2,1)S(1)} %shard_map.90.codes_ref, f32[512,256]{1,0:T(8,128)S(1)} %get-tuple-element.47.refs_0_, bf16[208,512]{1,0:T(8,128)(2,1)S(1)} %collective-permute-done.3.refs_3_.refs_1_, ...), custom_call_target="tpu_custom_call" | custom-call | flops 100000000 | bytes 1000000 | tf_op jit(solution)/shard_map/pallas_call | solution.py:35
  43.6 2.8 %collective-permute-start.24 = (bf16[192,512]{1,0:T(8,128)(2,1)S(1)}, bf16[192,512]{1,0:T(8,128)(2,1)S(1)}, u32[]{:S(2)}, u32[]{:S(2)}) collective-permute-start(bf16[192,512]{1,0:T(8,128)(2,1)S(1)} %get-tuple-element.59), channel_id=1, source_target_pairs={{0,24},{4,28},{8,16},{12,20},{16,8},{20,12},{24,0},{28,4},{1,25},{... | collective-permute-start | bytes 589832 | tf_op jit(solution)/shard_map/ppermute | solution.py:327
  47.2 1.9 %collective-permute-start.15 = (bf16[256,256]{1,0:T(8,128)(2,1)S(1)}, bf16[256,256]{1,0:T(8,128)(2,1)S(1)}, u32[]{:S(2)}, u32[]{:S(2)}) collective-permute-start(bf16[256,256]{1,0:T(8,128)(2,1)S(1)} %shard_map.94.refs_2_), channel_id=1, source_target_pairs={{0,8},{4,12},{8,0},{12,4},{16,24},{20,28},{24,16},{28,20},{1,9},{5... | collective-permute-start | bytes 393224 | tf_op jit(solution)/shard_map/ppermute | solution.py:327
  49.1 3.2 %collective-permute-done.24.refs_3_ = bf16[192,512]{1,0:T(8,128)(2,1)S(1)} collective-permute-done((bf16[192,512]{1,0:T(8,128)(2,1)S(1)}, bf16[192,512]{1,0:T(8,128)(2,1)S(1)}, u32[]{:S(2)}, u32[]{:S(2)}) %collective-permute-start.24) | collective-permute-done | bytes 196640 | tf_op jit(solution)/shard_map/ppermute | solution.py:327
  52.4 2.0 %collective-permute-start.16 = (bf16[256,256]{1,0:T(8,128)(2,1)S(1)}, bf16[256,256]{1,0:T(8,128)(2,1)S(1)}, u32[]{:S(2)}, u32[]{:S(2)}) collective-permute-start(bf16[256,256]{1,0:T(8,128)(2,1)S(1)} %shard_map.94.refs_2_), channel_id=1, source_target_pairs={{0,16},{4,20},{8,24},{12,28},{16,0},{20,4},{24,8},{28,12},{1,17},{... | collective-permute-start | bytes 393224 | tf_op jit(solution)/shard_map/ppermute | solution.py:327
  54.4 2.7 %collective-permute-done.22.refs_1_ = bf16[192,512]{1,0:T(8,128)(2,1)S(1)} collective-permute-done((bf16[192,512]{1,0:T(8,128)(2,1)S(1)}, bf16[192,512]{1,0:T(8,128)(2,1)S(1)}, u32[]{:S(2)}, u32[]{:S(2)}) %collective-permute-start.22) | collective-permute-done | bytes 196640 | tf_op jit(solution)/shard_map/ppermute | solution.py:327
  57.1 1.3 %collective-permute-start.17 = (bf16[256,256]{1,0:T(8,128)(2,1)S(1)}, bf16[256,256]{1,0:T(8,128)(2,1)S(1)}, u32[]{:S(2)}, u32[]{:S(2)}) collective-permute-start(bf16[256,256]{1,0:T(8,128)(2,1)S(1)} %shard_map.94.refs_2_), channel_id=1, source_target_pairs={{0,24},{4,28},{8,16},{12,20},{16,8},{20,12},{24,0},{28,4},{1,25},{... | collective-permute-start | bytes 393224 | tf_op jit(solution)/shard_map/ppermute | solution.py:327
  59.1 3.6 %collective-permute-start.26 = (bf16[192,128]{1,0:T(8,128)(2,1)S(1)}, bf16[192,128]{1,0:T(8,128)(2,1)S(1)}, u32[]{:S(2)}, u32[]{:S(2)}) collective-permute-start(bf16[192,128]{1,0:T(8,128)(2,1)S(1)} %get-tuple-element.62), channel_id=1, source_target_pairs={{0,2},{1,3},{2,0},{3,1},{4,6},{5,7},{6,4},{7,5},{8,10},{9,11},{10,... | collective-permute-start | bytes 147464 | tf_op jit(solution)/shard_map/ppermute | solution.py:324
  67.3 1.5 %collective-permute-start.21 = (bf16[208,128]{1,0:T(8,128)(2,1)S(1)}, bf16[208,128]{1,0:T(8,128)(2,1)S(1)}, u32[]{:S(2)}, u32[]{:S(2)}) collective-permute-start(bf16[208,128]{1,0:T(8,128)(2,1)S(1)} %get-tuple-element.53), channel_id=1, source_target_pairs={{0,5},{1,4},{2,7},{3,6},{4,3},{5,2},{6,1},{7,0},{8,13},{9,12},{10,... | collective-permute-start | bytes 159752 | tf_op jit(solution)/shard_map/ppermute | solution.py:337
  70.1 1.4 %shard_map.98 = bf16[192,2048]{1,0:T(8,128)(2,1)} custom-call(s32[4,4]{1,0:T(4,128)S(1)} %copy-done.6, bf16[192,2048]{1,0:T(8,128)(2,1)} %get-tuple-element.55.zero_ref, bf16[192,128]{1,0:T(8,128)(2,1)S(1)} %get-tuple-element.60.refs_0_, bf16[192,128]{1,0:T(8,128)(2,1)S(1)} %collective-permute-done.25.refs_1_, ...), custom_call_target="tpu_custom_call", output_to_operand_aliasing={{}: (1, {})} | custom-call | flops 100000000 | bytes 1000000 | tf_op jit(solution)/shard_map/pallas_call | solution.py:35
  73.0 2.0 %shard_map.96 = (bf16[192,2048]{1,0:T(8,128)(2,1)}, f32[1,2048]{1,0:T(1,128)}) custom-call(s32[4,4]{1,0:T(4,128)S(1)} %copy-done.6, bf16[192,2048]{1,0:T(8,128)(2,1)} %get-tuple-element.34.zero_ref, bf16[208,128]{1,0:T(8,128)(2,1)S(1)} %collective-permute-done.18.refs_0_, ...), custom_call_target="tpu_custom_call", output_to_operand_aliasing={{0}: (1, {})} | custom-call | flops 100000000 | bytes 1000000 | tf_op jit(solution)/shard_map/pallas_call | solution.py:35
  (63 shorter events, 21.5 us)
Async XLA Ops:
  6.2 18.2 %collective-permute-start.1 = (bf16[208,512]{1,0:T(8,128)(2,1)S(1)}, bf16[208,512]{1,0:T(8,128)(2,1)S(1)}, u32[]{:S(2)}, u32[]{:S(2)}) collective-permute-start(bf16[208,512]{1,0:T(8,128)(2,1)S(1)} %get-tuple-element.36), channel_id=1, source_target_pairs={{0,8},{4,12},{8,0},{12,4},{16,24},{20,28},{24,16},{28,20},{1,9},{5... | collective-permute-start | bytes 638984 | tf_op jit(solution)/shard_map/ppermute | solution.py:327
  10.0 6.0 %collective-permute-start.4 = (bf16[400,128]{1,0:T(8,128)(2,1)S(1)}, bf16[400,128]{1,0:T(8,128)(2,1)S(1)}, u32[]{:S(2)}, u32[]{:S(2)}) collective-permute-start(bf16[400,128]{1,0:T(8,128)(2,1)S(1)} %get-tuple-element.40), channel_id=1, source_target_pairs={{0,1},{1,0},{2,3},{3,2},{4,5},{5,4},{6,7},{7,6},{8,9},{9,8},{10,11... | collective-permute-start | bytes 307208 | tf_op jit(solution)/shard_map/ppermute | solution.py:324
  11.7 10.4 %collective-permute-start.5 = (bf16[400,128]{1,0:T(8,128)(2,1)S(1)}, bf16[400,128]{1,0:T(8,128)(2,1)S(1)}, u32[]{:S(2)}, u32[]{:S(2)}) collective-permute-start(bf16[400,128]{1,0:T(8,128)(2,1)S(1)} %get-tuple-element.41), channel_id=1, source_target_pairs={{0,2},{1,3},{2,0},{3,1},{4,6},{5,7},{6,4},{7,5},{8,10},{9,11},{10,... | collective-permute-start | bytes 307208 | tf_op jit(solution)/shard_map/ppermute | solution.py:324
  14.3 7.9 %collective-permute-start.6 = (bf16[400,128]{1,0:T(8,128)(2,1)S(1)}, bf16[400,128]{1,0:T(8,128)(2,1)S(1)}, u32[]{:S(2)}, u32[]{:S(2)}) collective-permute-start(bf16[400,128]{1,0:T(8,128)(2,1)S(1)} %get-tuple-element.42), channel_id=1, source_target_pairs={{0,3},{1,2},{2,1},{3,0},{4,7},{5,6},{6,5},{7,4},{8,11},{9,10},{10,... | collective-permute-start | bytes 307208 | tf_op jit(solution)/shard_map/ppermute | solution.py:324
  14.5 13.7 %collective-permute-start.2 = (bf16[208,512]{1,0:T(8,128)(2,1)S(1)}, bf16[208,512]{1,0:T(8,128)(2,1)S(1)}, u32[]{:S(2)}, u32[]{:S(2)}) collective-permute-start(bf16[208,512]{1,0:T(8,128)(2,1)S(1)} %get-tuple-element.37), channel_id=1, source_target_pairs={{0,16},{4,20},{8,24},{12,28},{16,0},{20,4},{24,8},{28,12},{1,17},{... | collective-permute-start | bytes 638984 | tf_op jit(solution)/shard_map/ppermute | solution.py:327
  16.0 12.1 %collective-permute-start.3 = (bf16[208,512]{1,0:T(8,128)(2,1)S(1)}, bf16[208,512]{1,0:T(8,128)(2,1)S(1)}, u32[]{:S(2)}, u32[]{:S(2)}) collective-permute-start(bf16[208,512]{1,0:T(8,128)(2,1)S(1)} %get-tuple-element.38), channel_id=1, source_target_pairs={{0,24},{4,28},{8,16},{12,20},{16,8},{20,12},{24,0},{28,4},{1,25},{... | collective-permute-start | bytes 638984 | tf_op jit(solution)/shard_map/ppermute | solution.py:327
  22.9 8.4 %collective-permute-start.8 = (bf16[192,384]{1,0:T(8,128)(2,1)S(1)}, bf16[192,384]{1,0:T(8,128)(2,1)S(1)}, u32[]{:S(2)}, u32[]{:S(2)}) collective-permute-start(bf16[192,384]{1,0:T(8,128)(2,1)S(1)} %get-tuple-element.43.refs_4_), channel_id=1, source_target_pairs={{0,16},{4,20},{8,24},{12,28},{16,0},{20,4},{24,8},{28,12},{1,17},{... | collective-permute-start | bytes 442376 | tf_op jit(solution)/shard_map/ppermute | solution.py:327
  24.4 6.9 %collective-permute-start.9 = (bf16[192,384]{1,0:T(8,128)(2,1)S(1)}, bf16[192,384]{1,0:T(8,128)(2,1)S(1)}, u32[]{:S(2)}, u32[]{:S(2)}) collective-permute-start(bf16[192,384]{1,0:T(8,128)(2,1)S(1)} %get-tuple-element.43.refs_4_), channel_id=1, source_target_pairs={{0,24},{4,28},{8,16},{12,20},{16,8},{20,12},{24,0},{28,4},{1,25},{... | collective-permute-start | bytes 442376 | tf_op jit(solution)/shard_map/ppermute | solution.py:327
  31.9 6.8 %collective-permute-start.11 = (bf16[192,384]{1,0:T(8,128)(2,1)S(1)}, bf16[192,384]{1,0:T(8,128)(2,1)S(1)}, u32[]{:S(2)}, u32[]{:S(2)}) collective-permute-start(bf16[192,384]{1,0:T(8,128)(2,1)S(1)} %get-tuple-element.45.refs_1_), channel_id=1, source_target_pairs={{0,8},{4,12},{8,0},{12,4},{16,24},{20,28},{24,16},{28,20},{1,9},{5... | collective-permute-start | bytes 442376 | tf_op jit(solution)/shard_map/ppermute | solution.py:327
  32.6 8.1 %collective-permute-start.12 = (bf16[192,384]{1,0:T(8,128)(2,1)S(1)}, bf16[192,384]{1,0:T(8,128)(2,1)S(1)}, u32[]{:S(2)}, u32[]{:S(2)}) collective-permute-start(bf16[192,384]{1,0:T(8,128)(2,1)S(1)} %get-tuple-element.45.refs_1_), channel_id=1, source_target_pairs={{0,16},{4,20},{8,24},{12,28},{16,0},{20,4},{24,8},{28,12},{1,17},{... | collective-permute-start | bytes 442376 | tf_op jit(solution)/shard_map/ppermute | solution.py:327
  34.1 8.1 %collective-permute-start.13 = (bf16[192,384]{1,0:T(8,128)(2,1)S(1)}, bf16[192,384]{1,0:T(8,128)(2,1)S(1)}, u32[]{:S(2)}, u32[]{:S(2)}) collective-permute-start(bf16[192,384]{1,0:T(8,128)(2,1)S(1)} %get-tuple-element.45.refs_1_), channel_id=1, source_target_pairs={{0,24},{4,28},{8,16},{12,20},{16,8},{20,12},{24,0},{28,4},{1,25},{... | collective-permute-start | bytes 442376 | tf_op jit(solution)/shard_map/ppermute | solution.py:327
  35.4 23.7 %collective-permute-start = (bf16[192,1024]{1,0:T(8,128)(2,1)S(1)}, bf16[192,1024]{1,0:T(8,128)(2,1)S(1)}, u32[]{:S(2)}, u32[]{:S(2)}) collective-permute-start(bf16[192,1024]{1,0:T(8,128)(2,1)S(1)} %copy-done.5), channel_id=1, source_target_pairs={{0,4},{4,0},{8,12},{12,8},{16,20},{20,16},{24,28},{28,24},{1,5},{5... | collective-permute-start | bytes 1179656 | tf_op jit(solution)/shard_map/ppermute | solution.py:327
  43.6 8.7 %collective-permute-start.24 = (bf16[192,512]{1,0:T(8,128)(2,1)S(1)}, bf16[192,512]{1,0:T(8,128)(2,1)S(1)}, u32[]{:S(2)}, u32[]{:S(2)}) collective-permute-start(bf16[192,512]{1,0:T(8,128)(2,1)S(1)} %get-tuple-element.59), channel_id=1, source_target_pairs={{0,24},{4,28},{8,16},{12,20},{16,8},{20,12},{24,0},{28,4},{1,25},{... | collective-permute-start | bytes 589832 | tf_op jit(solution)/shard_map/ppermute | solution.py:327
  46.5 10.7 %collective-permute-start.22 = (bf16[192,512]{1,0:T(8,128)(2,1)S(1)}, bf16[192,512]{1,0:T(8,128)(2,1)S(1)}, u32[]{:S(2)}, u32[]{:S(2)}) collective-permute-start(bf16[192,512]{1,0:T(8,128)(2,1)S(1)} %get-tuple-element.57), channel_id=1, source_target_pairs={{0,8},{4,12},{8,0},{12,4},{16,24},{20,28},{24,16},{28,20},{1,9},{5... | collective-permute-start | bytes 589832 | tf_op jit(solution)/shard_map/ppermute | solution.py:327
  47.1 11.3 %collective-permute-start.23 = (bf16[192,512]{1,0:T(8,128)(2,1)S(1)}, bf16[192,512]{1,0:T(8,128)(2,1)S(1)}, u32[]{:S(2)}, u32[]{:S(2)}) collective-permute-start(bf16[192,512]{1,0:T(8,128)(2,1)S(1)} %get-tuple-element.58), channel_id=1, source_target_pairs={{0,16},{4,20},{8,24},{12,28},{16,0},{20,4},{24,8},{28,12},{1,17},{... | collective-permute-start | bytes 589832 | tf_op jit(solution)/shard_map/ppermute | solution.py:327
  47.2 15.5 %collective-permute-start.15 = (bf16[256,256]{1,0:T(8,128)(2,1)S(1)}, bf16[256,256]{1,0:T(8,128)(2,1)S(1)}, u32[]{:S(2)}, u32[]{:S(2)}) collective-permute-start(bf16[256,256]{1,0:T(8,128)(2,1)S(1)} %shard_map.94.refs_2_), channel_id=1, source_target_pairs={{0,8},{4,12},{8,0},{12,4},{16,24},{20,28},{24,16},{28,20},{1,9},{5... | collective-permute-start | bytes 393224 | tf_op jit(solution)/shard_map/ppermute | solution.py:327
  52.4 11.1 %collective-permute-start.16 = (bf16[256,256]{1,0:T(8,128)(2,1)S(1)}, bf16[256,256]{1,0:T(8,128)(2,1)S(1)}, u32[]{:S(2)}, u32[]{:S(2)}) collective-permute-start(bf16[256,256]{1,0:T(8,128)(2,1)S(1)} %shard_map.94.refs_2_), channel_id=1, source_target_pairs={{0,16},{4,20},{8,24},{12,28},{16,0},{20,4},{24,8},{28,12},{1,17},{... | collective-permute-start | bytes 393224 | tf_op jit(solution)/shard_map/ppermute | solution.py:327
  57.1 6.4 %collective-permute-start.17 = (bf16[256,256]{1,0:T(8,128)(2,1)S(1)}, bf16[256,256]{1,0:T(8,128)(2,1)S(1)}, u32[]{:S(2)}, u32[]{:S(2)}) collective-permute-start(bf16[256,256]{1,0:T(8,128)(2,1)S(1)} %shard_map.94.refs_2_), channel_id=1, source_target_pairs={{0,24},{4,28},{8,16},{12,20},{16,8},{20,12},{24,0},{28,4},{1,25},{... | collective-permute-start | bytes 393224 | tf_op jit(solution)/shard_map/ppermute | solution.py:327
  58.5 7.6 %collective-permute-start.25 = (bf16[192,128]{1,0:T(8,128)(2,1)S(1)}, bf16[192,128]{1,0:T(8,128)(2,1)S(1)}, u32[]{:S(2)}, u32[]{:S(2)}) collective-permute-start(bf16[192,128]{1,0:T(8,128)(2,1)S(1)} %get-tuple-element.61), channel_id=1, source_target_pairs={{0,1},{1,0},{2,3},{3,2},{4,5},{5,4},{6,7},{7,6},{8,9},{9,8},{10,11... | collective-permute-start | bytes 147464 | tf_op jit(solution)/shard_map/ppermute | solution.py:324
  59.1 8.2 %collective-permute-start.26 = (bf16[192,128]{1,0:T(8,128)(2,1)S(1)}, bf16[192,128]{1,0:T(8,128)(2,1)S(1)}, u32[]{:S(2)}, u32[]{:S(2)}) collective-permute-start(bf16[192,128]{1,0:T(8,128)(2,1)S(1)} %get-tuple-element.62), channel_id=1, source_target_pairs={{0,2},{1,3},{2,0},{3,1},{4,6},{5,7},{6,4},{7,5},{8,10},{9,11},{10,... | collective-permute-start | bytes 147464 | tf_op jit(solution)/shard_map/ppermute | solution.py:324
  62.7 7.4 %collective-permute-start.27 = (bf16[192,128]{1,0:T(8,128)(2,1)S(1)}, bf16[192,128]{1,0:T(8,128)(2,1)S(1)}, u32[]{:S(2)}, u32[]{:S(2)}) collective-permute-start(bf16[192,128]{1,0:T(8,128)(2,1)S(1)} %get-tuple-element.63), channel_id=1, source_target_pairs={{0,3},{1,2},{2,1},{3,0},{4,7},{5,6},{6,5},{7,4},{8,11},{9,10},{10,... | collective-permute-start | bytes 147464 | tf_op jit(solution)/shard_map/ppermute | solution.py:324
  64.2 7.3 %collective-permute-start.18 = (bf16[208,128]{1,0:T(8,128)(2,1)S(1)}, bf16[208,128]{1,0:T(8,128)(2,1)S(1)}, u32[]{:S(2)}, u32[]{:S(2)}) collective-permute-start(bf16[208,128]{1,0:T(8,128)(2,1)S(1)} %get-tuple-element.50), channel_id=1, source_target_pairs={{0,0},{1,1},{2,2},{3,3},{4,6},{5,7},{6,4},{7,5},{8,8},{9,9},{10,10... | collective-permute-start | bytes 159752 | tf_op jit(solution)/shard_map/ppermute | solution.py:337
  64.9 6.6 %collective-permute-start.19 = (bf16[208,128]{1,0:T(8,128)(2,1)S(1)}, bf16[208,128]{1,0:T(8,128)(2,1)S(1)}, u32[]{:S(2)}, u32[]{:S(2)}) collective-permute-start(bf16[208,128]{1,0:T(8,128)(2,1)S(1)} %get-tuple-element.51), channel_id=1, source_target_pairs={{0,1},{1,0},{2,3},{3,2},{4,7},{5,6},{6,5},{7,4},{8,9},{9,8},{10,11... | collective-permute-start | bytes 159752 | tf_op jit(solution)/shard_map/ppermute | solution.py:337
  66.1 6.0 %collective-permute-start.20 = (bf16[208,128]{1,0:T(8,128)(2,1)S(1)}, bf16[208,128]{1,0:T(8,128)(2,1)S(1)}, u32[]{:S(2)}, u32[]{:S(2)}) collective-permute-start(bf16[208,128]{1,0:T(8,128)(2,1)S(1)} %get-tuple-element.52), channel_id=1, source_target_pairs={{0,4},{1,5},{2,6},{3,7},{4,2},{5,3},{6,0},{7,1},{8,12},{9,13},{10,... | collective-permute-start | bytes 159752 | tf_op jit(solution)/shard_map/ppermute | solution.py:337
  (12 other events, 35.4 us)

commit v2 on v1

--- a/solution.py
+++ b/solution.py
@@ -25,6 +25,10 @@
 
 def anywhere():
     return pl.BlockSpec(memory_space=pl.ANY)
+
+
+def in_hbm(x):
+    return pltpu.with_memory_space_constraint(x, pltpu.HBM)
 
 
 def dot(a, b, da, db):
@@ -77,42 +81,38 @@
     return lanes(jnp.maximum(tile, 0), TILE)
 
 
-def first_kernel(owners, tiles, parts, ids_ref, enc_ref, dec_ref, bias_ref, *rest):
-    outs, sem = rest[:-1], rest[-1]
-    features = enc_ref.shape[0]
-    me, _, _ = place(parts)
-    copies = []
-    for step in range(1, owners):
-        where = send_lanes(ids_ref, me, step, tiles)
-        for index, source in enumerate((enc_ref, dec_ref)):
-            target = outs[step - 1].at[pl.ds(index * features, features), :]
-            copies.append(pltpu.make_async_copy(source.at[:, where], target, sem.at[len(copies)]))
-    for copy in copies:
-        copy.start()
-    for step in range(1, owners):
-        bias = bias_ref[:, send_lanes(ids_ref, me, step, tiles)]
-        outs[step - 1][pl.ds(2 * features, EXTRA), :] = jnp.broadcast_to(bias, (EXTRA, TILE))
-    for copy in copies:
-        copy.wait()
-
-
-def second_kernel(tiles, parts, ids_ref, acts_ref, enc_ref, dec_ref, bias_ref, offset_ref, *rest):
-    messages, bias_out, sem = rest[:parts], rest[-2], rest[-1]
+def bias_rows(ids_ref, bias_ref, me, step):
+    tiles = bias_ref.shape[0]
+    tile = wanted_tile(ids_ref, xor(me, step), me, tiles)
+    row = lax.broadcasted_iota(jnp.int32, bias_ref.shape, 0)
+    picked = jnp.where(row == tile, bias_ref[...].astype(F32), 0.0)
+    line = jnp.sum(picked, axis=0, keepdims=True)
+    live = jnp.where(tile >= 0, 1.0, 0.0)
+    row = lax.broadcasted_iota(jnp.int32, (EXTRA, TILE), 0)
+    return jnp.where(row == 0, line, live).astype(BF16)
+
+
+def pack_kernel(owners, tiles, parts, ids_ref, acts_ref, enc_ref, dec_ref, bias_ref, offset_ref, *rest):
+    moved, messages, bias_out, sem = rest[: owners - 1], rest[owners - 1 : -2], rest[-2], rest[-1]
     features, rows = acts_ref.shape
     quarter = rows // parts
     me, part, _ = place(parts)
     inner = pl.ds(0, features)
+    pairs = []
+    for step in range(1, owners):
+        where = send_lanes(ids_ref, me, step, tiles)
+        for index, source in enumerate((enc_ref, dec_ref)):
+            target = moved[step - 1].at[pl.ds(index * features, features), :]
+            pairs.append((source.at[:, where], target))
     here = send_lanes(ids_ref, me, 0, tiles)
-    copies = []
     for step in range(parts):
-        out = messages[step]
         acts = acts_ref.at[:, lanes(xor(part, step), quarter)]
         start = 0
         for source in (acts, enc_ref.at[:, here], dec_ref.at[:, here]):
             size = source.shape[1]
-            target = out.at[inner, pl.ds(start, size)]
-            copies.append(pltpu.make_async_copy(source, target, sem.at[len(copies)]))
+            pairs.append((source, messages[step].at[inner, pl.ds(start, size)]))
             start += size
+    copies = [pltpu.make_async_copy(a, b, sem.at[i]) for i, (a, b) in enumerate(pairs)]
     for copy in copies:
         copy.start()
     offset = offset_ref[...]
@@ -127,7 +127,9 @@
     for step in range(parts):
         messages[step][pl.ds(features, EXTRA), :] = jnp.zeros((EXTRA, quarter + 2 * TILE), BF16)
         messages[step][pl.ds(features, EXTRA), pl.ds(0, features)] = split
-    bias_out[...] = jnp.broadcast_to(bias_ref[:, here], (EXTRA, TILE))
+    for step in range(1, owners):
+        moved[step - 1][pl.ds(2 * features, EXTRA), :] = bias_rows(ids_ref, bias_ref, me, step)
+    bias_out[...] = bias_rows(ids_ref, bias_ref, me, 0)
     for copy in copies:
         copy.wait()
 
@@ -173,22 +175,24 @@
     out_ref[pl.ds(TILE, out_ref.shape[0] - TILE), :] = two
 
 
-def codes_kernel(owners, tiles, parts, ids_ref, mine_ref, other_ref, bias_ref, out_ref):
-    me, _, _ = place(parts)
-    quarter = out_ref.shape[1]
+def codes_of(mine_ref, other_ref, bias_ref):
+    quarter = mine_ref.shape[1]
     row = lax.broadcasted_iota(jnp.int32, (EXTRA, quarter), 0)
-    pick = jnp.where(row == 0, 1.0, 0.0).astype(BF16)
-    for step in range(owners):
-        live = wanted_tile(ids_ref, me, xor(me, step), tiles) >= 0
-        where = pl.ds(step * TILE, TILE)
-        bias = dot(bias_ref[:, where], pick, 0, 0)
-        pre = mine_ref[where, :] + other_ref[where, :] + bias
-        out_ref[where, :] = jnp.where(live, jnp.maximum(pre, 0.0), 0.0).astype(BF16)
-
-
-def decode_kernel(count, cores, parts, scale, first, last, codes_ref, *refs):
+    bias = dot(bias_ref[...], jnp.where(row == 0, 1.0, 0.0).astype(BF16), 0, 0)
+    live = dot(bias_ref[...], jnp.where(row == 1, 1.0, 0.0).astype(BF16), 0, 0)
+    pre = mine_ref[...] + other_ref[...] + bias
+    return (jnp.maximum(pre, 0.0) * live).astype(BF16)
+
+
+def decode_kernel(count, cores, parts, scale, first, last, *refs):
     refs = list(refs)
-    before = None if first else refs.pop(0)
+    if first:
+        sources = [refs.pop(0) for _ in range(3)]
+        codes_ref = refs.pop(2 * count)
+        codes_ref[...] = codes_of(*sources)
+        before = None
+    else:
+        codes_ref, before = refs.pop(0), refs.pop(0)
     messages, decs = refs[:count], refs[count : 2 * count]
     grads = refs[2 * count : 3 * count]
     outs = refs[3 * count :]
@@ -212,14 +216,23 @@
         right = dot(dec, err, 0, 0).astype(BF16).astype(F32)
         one = left if one is None else one + left
         two = right if two is None else two + right
-    total = outs[-1]
-    total[pl.ds(0, TILE), :] = one
-    total[pl.ds(TILE, width - TILE), :] = two
     if last:
         _, _, core = place(parts)
         half = width // cores
+        hold = outs[-1]
+        for block in range(cores):
+            start, stop = block * half, (block + 1) * half
+            if start == 0:
+                hold[xor(core, block), pl.ds(0, TILE), :] = one
+                hold[xor(core, block), pl.ds(TILE, half - TILE), :] = two[: half - TILE]
+            else:
+                hold[xor(core, block)] = two[start - TILE : stop - TILE]
         for step in range(cores):
-            outs[step][...] = total[lanes(xor(core, step), half), :]
+            outs[step][...] = hold[step]
+    else:
+        total = outs[-1]
+        total[pl.ds(0, TILE), :] = one
+        total[pl.ds(TILE, width - TILE), :] = two
 
 
 def mask_kernel(parts, codes_ref, *refs):
@@ -272,7 +285,9 @@
         slot = xor(core, step // share) * share + step % share if crossed else step
         found.append(wanted_tile(ids_ref, xor(me, slot), me, tiles))
     if crossed:
-        refs[owners + 1][...] = jnp.zeros_like(refs[owners + 1])
+        bias_out, bias_hold, bias_sem = refs[owners + 1], refs[-4], refs[-3]
+        bias_hold[...] = jnp.zeros_like(bias_hold)
+        bias_copy = pltpu.make_async_copy(bias_hold, bias_out, bias_sem)
     fresh = []
     for step in range(owners):
         new = found[step] >= 0
@@ -280,29 +295,48 @@
             new = new & (found[peer] != found[step])
         fresh.append(new)
 
-    def copy(step):
+    def copy(step, source):
         where = lanes(jnp.maximum(found[step], 0), TILE)
-        return pltpu.make_async_copy(hold.at[step], out_ref.at[:, where], sem.at[step])
-
+        return pltpu.make_async_copy(source, out_ref.at[:, where], sem.at[step])
+
+    for step in range(owners):
+        again = jnp.bool_(False)
+        for peer in range(step + 1, owners):
+            again = again | (found[peer] == found[step])
+
+        @pl.when(fresh[step] & jnp.logical_not(again))
+        def _():
+            copy(step, got[step].at[pl.ds(0, features), :]).start()
+
+        @pl.when(fresh[step] & again)
+        def _():
+            total = got[step][pl.ds(0, features), :].astype(F32)
+            for peer in range(step + 1, owners):
+                same = got[peer][pl.ds(0, features), :].astype(F32)
+                total = total + jnp.where(found[peer] == found[step], same, 0.0)
+            hold[step] = total.astype(BF16)
+            copy(step, hold.at[step]).start()
+
+        if crossed:
+
+            @pl.when(fresh[step])
+            def _():
+                total = got[step][pl.ds(features, EXTRA), :].astype(F32)
+                for peer in range(step + 1, owners):
+                    same = got[peer][pl.ds(features, EXTRA), :].astype(F32)
+                    total = total + jnp.where(found[peer] == found[step], same, 0.0)
+                bias_hold[:, lanes(found[step], TILE)] = total[:1]
+
+    if crossed:
+        bias_copy.start()
     for step in range(owners):
 
         @pl.when(fresh[step])
         def _():
-            total = got[step][...].astype(F32)
-            for peer in range(step + 1, owners):
-                total = total + jnp.where(
-                    found[peer] == found[step], got[peer][...].astype(F32), 0.0
-                )
-            hold[step] = total[:features].astype(BF16)
-            copy(step).start()
-            if crossed:
-                refs[owners + 1][:, lanes(found[step], TILE)] = total[features : features + 1]
-
-    for step in range(owners):
-
-        @pl.when(fresh[step])
-        def _():
-            copy(step).wait()
+            copy(step, hold.at[step]).wait()
+
+    if crossed:
+        bias_copy.wait()
 
 
 def sizes(mesh):
@@ -339,22 +373,24 @@
     def gather(x):
         return [x] + [over_layer(x, s, cores) for s in range(1, parts)]
 
-    bias_line = b_enc.reshape(1, latents)
-    moved = call(
-        functools.partial(first_kernel, owners, tiles, parts),
-        [shape(2 * features + EXTRA, TILE)] * (owners - 1),
-        [smem(), anywhere(), anywhere(), vmem()],
-        (tile_ids, w_enc, w_dec, bias_line),
-        scratch=[pltpu.SemaphoreType.DMA((2 * (owners - 1),))],
-    )
-    second = call(
-        functools.partial(second_kernel, tiles, parts),
-        [shape(features + EXTRA, quarter + 2 * TILE)] * parts + [shape(EXTRA, TILE)],
+    bias_line = b_enc.reshape(tiles, TILE)
+    packed = call(
+        functools.partial(pack_kernel, owners, tiles, parts),
+        [shape(2 * features + EXTRA, TILE)] * (owners - 1)
+        + [shape(features + EXTRA, quarter + 2 * TILE)] * parts
+        + [shape(EXTRA, TILE)],
         [smem(), anywhere(), anywhere(), anywhere(), vmem(), vmem()],
-        (tile_ids, activations, w_enc, w_dec, bias_line, b_dec.reshape(1, features)),
-        scratch=[pltpu.SemaphoreType.DMA((3 * parts,))],
-    )
-    messages, own_bias = second[:parts], second[-1]
+        (
+            in_hbm(tile_ids),
+            in_hbm(activations),
+            in_hbm(w_enc),
+            in_hbm(w_dec),
+            in_hbm(bias_line),
+            in_hbm(b_dec.reshape(1, features)),
+        ),
+        scratch=[pltpu.SemaphoreType.DMA((3 * parts + 2 * (owners - 1),))],
+    )
+    moved, messages, own_bias = packed[: owners - 1], packed[owners - 1 : -1], packed[-1]
     moved = [over_lat(x, s + 1) for s, x in enumerate(moved)]
     messages = [messages[0]] + [over_layer(messages[s], s, cores) for s in range(1, parts)]
     all_acts = [activations] + [over_layer(activations, s, 1) for s in range(1, cores)]
@@ -378,21 +414,18 @@
         mine = mine + over_layer(mine, step, 1)
         step = 2 * step
     other = over_layer(mine, step, 1)
-    codes = call(
-        functools.partial(codes_kernel, owners, tiles, parts),
-        shape(width, quarter),
-        [smem()] + [vmem()] * 3,
-        (tile_ids, mine, other, bias_rows),
-    )
     groups = [[0], list(range(1, parts - 1)), [parts - 1]]
     total, sent = None, []
     for index, group in enumerate(groups):
         first, last = index == 0, index == len(groups) - 1
-        outs = [shape(features, width)] * len(group)
+        outs = [shape(width, quarter)] if first else []
+        outs += [shape(features, width)] * len(group)
+        scratch = [pltpu.VMEM((cores, half, quarter), F32)] if last else []
         if last:
             outs += [shape(half, quarter, kind=F32)] * cores
-        outs += [shape(width, quarter, kind=F32)]
-        args = [codes] + ([] if first else [total])
+        else:
+            outs += [shape(width, quarter, kind=F32)]
+        args = [mine, other, bias_rows] if first else [codes, total]
         args += [messages[s] for s in group] + [decs[s] for s in group]
         out = call(
             functools.partial(
@@ -401,10 +434,13 @@
             outs,
             [vmem()] * len(args),
             tuple(args),
+            scratch=scratch,
         )
+        if first:
+            codes, out = out[0], out[1:]
         sent += out[: len(group)]
         total = out[-1]
-        sums = out[len(group) : -1]
+        sums = out[len(group) :]
     sums = [sums[0]] + [over_layer(sums[s], s, 1) for s in range(1, cores)]
     grad = call(
         functools.partial(mask_kernel, parts),
@@ -448,8 +484,9 @@
             outs,
             [smem(), anywhere()] + [vmem()] * owners,
             (tile_ids, zero, *pieces),
-            out_specs=[anywhere()] + ([vmem()] if cross else []),
-            scratch=[pltpu.VMEM((owners, features, TILE), BF16), pltpu.SemaphoreType.DMA((owners,))],
+            out_specs=[anywhere()] * len(outs),
+            scratch=([pltpu.VMEM((1, latents), F32), pltpu.SemaphoreType.DMA] if cross else [])
+            + [pltpu.VMEM((owners, features, TILE), BF16), pltpu.SemaphoreType.DMA((owners,))],
             alias={1: 0},
         )
 

time: 75.2 us -> 69.7 us (0.927)
  local copies, waits for them, and re-layouts: 4.65 us -> 0.67 us
  Pallas kernels: 11.5 us -> 10.1 us
    unnamed x16 -> x4, local copies, waits for them, and re-layouts: 3.95 us -> 0.67 us
    pallas_call x14 -> x12, Pallas kernels: 11.5 us -> 10.1 us  [call(): pl.pallas_call(kernel, out_shape=outs, in_specs=ins, out_specs=jax.tree.m...]
  transfers between devices with their start and end apart: 28 -> 28, of which waited for: 10 -> 10; matrix products, arithmetic and copies ran while one was open for 0% -> 0% of each run, Pallas kernels for 11% -> 9%
where the time goes in v2:
time: 69.7 us; the launch traced here: 69.5 us
  starting transfers between devices  35.8 us (51%)
  waiting for transfers between devices  22.2 us (32%)
  Pallas kernels  10.1 us (14%)
  between operations  0.79 us (1%)
    ppermute x18, starting transfers between devices, over_layer(): lax.ppermute(x, 'layer', [(i, i ^ step * stride) for i in range(layers)])  21.9 us
    ppermute x18, waiting for transfers between devices, over_layer(): lax.ppermute(x, 'layer', [(i, i ^ step * stride) for i in range(layers)])  16.5 us
    pallas_call x12, Pallas kernels, call(): pl.pallas_call(kernel, out_shape=outs, in_specs=ins, out_specs=jax.tree.m...  10.1 us
    ppermute x6, starting transfers between devices, over_lat(): return lax.ppermute(x, 'lat', [(i, i ^ step) for i in range(owners)])  9.19 us
    ppermute x6, waiting for transfers between devices, over_lat(): return lax.ppermute(x, 'lat', [(i, i ^ step) for i in range(owners)])  4.86 us
    ppermute x4, starting transfers between devices, crossed(): return lax.ppermute(x, ('layer', 'lat'), pairs)  4.71 us
  transfers between devices with their start and end apart: 28, of which 10 were waited for; matrix products, arithmetic and copies ran while one was open for 0% of the time, Pallas kernels for 9%

profile of v2, /device:TPU:0, one launch (start us, length us, event | category | flops | bytes accessed | tf_op | source)
XLA Modules:
  0.0 69.5 jit_solution(7127762521617826447)
XLA Ops:
  0.6 2.2 %shard_map.86 = (bf16[400,128]{1,0:T(8,128)(2,1)S(1)}, bf16[400,128]{1,0:T(8,128)(2,1)S(1)}, bf16[400,128]{1,0:T(8,128)(2,1)S(1)}, bf16[208,512]{1,0:T(8,128)(2,...) custom-call(s32[4,4]{1,0:T(4,128)} %ids_ref.5, ...), custom_call_target="tpu_custom_call" | custom-call | flops 100000000 | bytes 1000000 | tf_op jit(solution)/shard_map/pallas_call | solution.py:39
  2.9 3.0 %collective-permute-start.1 = (bf16[208,512]{1,0:T(8,128)(2,1)S(1)}, bf16[208,512]{1,0:T(8,128)(2,1)S(1)}, u32[]{:S(2)}, u32[]{:S(2)}) collective-permute-start(bf16[208,512]{1,0:T(8,128)(2,1)S(1)} %get-tuple-element.37), channel_id=1, source_target_pairs={{0,8},{4,12},{8,0},{12,4},{16,24},{20,28},{24,16},{28,20},{1,9},{5... | collective-permute-start | bytes 638984 | tf_op jit(solution)/shard_map/ppermute | solution.py:361
  5.9 1.6 %collective-permute-start.4 = (bf16[400,128]{1,0:T(8,128)(2,1)S(1)}, bf16[400,128]{1,0:T(8,128)(2,1)S(1)}, u32[]{:S(2)}, u32[]{:S(2)}) collective-permute-start(bf16[400,128]{1,0:T(8,128)(2,1)S(1)} %get-tuple-element.41), channel_id=1, source_target_pairs={{0,1},{1,0},{2,3},{3,2},{4,5},{5,4},{6,7},{7,6},{8,9},{9,8},{10,11... | collective-permute-start | bytes 307208 | tf_op jit(solution)/shard_map/ppermute | solution.py:358
  7.5 2.6 %collective-permute-start.5 = (bf16[400,128]{1,0:T(8,128)(2,1)S(1)}, bf16[400,128]{1,0:T(8,128)(2,1)S(1)}, u32[]{:S(2)}, u32[]{:S(2)}) collective-permute-start(bf16[400,128]{1,0:T(8,128)(2,1)S(1)} %get-tuple-element.42), channel_id=1, source_target_pairs={{0,2},{1,3},{2,0},{3,1},{4,6},{5,7},{6,4},{7,5},{8,10},{9,11},{10,... | collective-permute-start | bytes 307208 | tf_op jit(solution)/shard_map/ppermute | solution.py:358
  10.3 1.5 %collective-permute-start.2 = (bf16[208,512]{1,0:T(8,128)(2,1)S(1)}, bf16[208,512]{1,0:T(8,128)(2,1)S(1)}, u32[]{:S(2)}, u32[]{:S(2)}) collective-permute-start(bf16[208,512]{1,0:T(8,128)(2,1)S(1)} %get-tuple-element.38), channel_id=1, source_target_pairs={{0,16},{4,20},{8,24},{12,28},{16,0},{20,4},{24,8},{28,12},{1,17},{... | collective-permute-start | bytes 638984 | tf_op jit(solution)/shard_map/ppermute | solution.py:361
  13.1 4.8 %collective-permute-done.5.refs_1_ = bf16[400,128]{1,0:T(8,128)(2,1)S(1)} collective-permute-done((bf16[400,128]{1,0:T(8,128)(2,1)S(1)}, bf16[400,128]{1,0:T(8,128)(2,1)S(1)}, u32[]{:S(2)}, u32[]{:S(2)}) %collective-permute-start.5) | collective-permute-done | bytes 102432 | tf_op jit(solution)/shard_map/ppermute | solution.py:358
  18.6 1.5 %collective-permute-start.8 = (bf16[192,384]{1,0:T(8,128)(2,1)S(1)}, bf16[192,384]{1,0:T(8,128)(2,1)S(1)}, u32[]{:S(2)}, u32[]{:S(2)}) collective-permute-start(bf16[192,384]{1,0:T(8,128)(2,1)S(1)} %get-tuple-element.44.refs_4_), channel_id=1, source_target_pairs={{0,16},{4,20},{8,24},{12,28},{16,0},{20,4},{24,8},{28,12},{1,17},{... | collective-permute-start | bytes 442376 | tf_op jit(solution)/shard_map/ppermute | solution.py:361
  20.1 1.4 %collective-permute-start.9 = (bf16[192,384]{1,0:T(8,128)(2,1)S(1)}, bf16[192,384]{1,0:T(8,128)(2,1)S(1)}, u32[]{:S(2)}, u32[]{:S(2)}) collective-permute-start(bf16[192,384]{1,0:T(8,128)(2,1)S(1)} %get-tuple-element.44.refs_4_), channel_id=1, source_target_pairs={{0,24},{4,28},{8,16},{12,20},{16,8},{20,12},{24,0},{28,4},{1,25},{... | collective-permute-start | bytes 442376 | tf_op jit(solution)/shard_map/ppermute | solution.py:361
  21.5 2.5 %collective-permute-done.2.refs_2_.refs_3_ = bf16[208,512]{1,0:T(8,128)(2,1)S(1)} collective-permute-done((bf16[208,512]{1,0:T(8,128)(2,1)S(1)}, bf16[208,512]{1,0:T(8,128)(2,1)S(1)}, u32[]{:S(2)}, u32[]{:S(2)}) %collective-permute-start.2) | collective-permute-done | bytes 213024 | tf_op jit(solution)/shard_map/ppermute | solution.py:361
  24.0 3.2 %collective-permute-done.8.refs_6_ = bf16[192,384]{1,0:T(8,128)(2,1)S(1)} collective-permute-done((bf16[192,384]{1,0:T(8,128)(2,1)S(1)}, bf16[192,384]{1,0:T(8,128)(2,1)S(1)}, u32[]{:S(2)}, u32[]{:S(2)}) %collective-permute-start.8) | collective-permute-done | bytes 147488 | tf_op jit(solution)/shard_map/ppermute | solution.py:361
  28.3 1.5 %collective-permute-start.12 = (bf16[192,384]{1,0:T(8,128)(2,1)S(1)}, bf16[192,384]{1,0:T(8,128)(2,1)S(1)}, u32[]{:S(2)}, u32[]{:S(2)}) collective-permute-start(bf16[192,384]{1,0:T(8,128)(2,1)S(1)} %get-tuple-element.46.refs_4_), channel_id=1, source_target_pairs={{0,16},{4,20},{8,24},{12,28},{16,0},{20,4},{24,8},{28,12},{1,17},{... | collective-permute-start | bytes 442376 | tf_op jit(solution)/shard_map/ppermute | solution.py:361
  29.8 1.4 %collective-permute-start.13 = (bf16[192,384]{1,0:T(8,128)(2,1)S(1)}, bf16[192,384]{1,0:T(8,128)(2,1)S(1)}, u32[]{:S(2)}, u32[]{:S(2)}) collective-permute-start(bf16[192,384]{1,0:T(8,128)(2,1)S(1)} %get-tuple-element.46.refs_4_), channel_id=1, source_target_pairs={{0,24},{4,28},{8,16},{12,20},{16,8},{20,12},{24,0},{28,4},{1,25},{... | collective-permute-start | bytes 442376 | tf_op jit(solution)/shard_map/ppermute | solution.py:361
  32.2 2.3 %collective-permute-done.11.refs_4_ = bf16[192,384]{1,0:T(8,128)(2,1)S(1)} collective-permute-done((bf16[192,384]{1,0:T(8,128)(2,1)S(1)}, bf16[192,384]{1,0:T(8,128)(2,1)S(1)}, u32[]{:S(2)}, u32[]{:S(2)}) %collective-permute-start.11) | collective-permute-done | bytes 147488 | tf_op jit(solution)/shard_map/ppermute | solution.py:361
  34.5 1.9 %collective-permute-done.12.refs_5_ = bf16[192,384]{1,0:T(8,128)(2,1)S(1)} collective-permute-done((bf16[192,384]{1,0:T(8,128)(2,1)S(1)}, bf16[192,384]{1,0:T(8,128)(2,1)S(1)}, u32[]{:S(2)}, u32[]{:S(2)}) %collective-permute-start.12) | collective-permute-done | bytes 147488 | tf_op jit(solution)/shard_map/ppermute | solution.py:361
  38.8 2.9 %collective-permute-start.24 = (bf16[192,512]{1,0:T(8,128)(2,1)S(1)}, bf16[192,512]{1,0:T(8,128)(2,1)S(1)}, u32[]{:S(2)}, u32[]{:S(2)}) collective-permute-start(bf16[192,512]{1,0:T(8,128)(2,1)S(1)} %get-tuple-element.61), channel_id=1, source_target_pairs={{0,24},{4,28},{8,16},{12,20},{16,8},{20,12},{24,0},{28,4},{1,25},{... | collective-permute-start | bytes 589832 | tf_op jit(solution)/shard_map/ppermute | solution.py:361
  42.4 1.9 %collective-permute-start.15 = (bf16[256,256]{1,0:T(8,128)(2,1)S(1)}, bf16[256,256]{1,0:T(8,128)(2,1)S(1)}, u32[]{:S(2)}, u32[]{:S(2)}) collective-permute-start(bf16[256,256]{1,0:T(8,128)(2,1)S(1)} %shard_map.92.refs_2_), channel_id=1, source_target_pairs={{0,8},{4,12},{8,0},{12,4},{16,24},{20,28},{24,16},{28,20},{1,9},{5... | collective-permute-start | bytes 393224 | tf_op jit(solution)/shard_map/ppermute | solution.py:361
  44.3 3.2 %collective-permute-done.24.refs_3_ = bf16[192,512]{1,0:T(8,128)(2,1)S(1)} collective-permute-done((bf16[192,512]{1,0:T(8,128)(2,1)S(1)}, bf16[192,512]{1,0:T(8,128)(2,1)S(1)}, u32[]{:S(2)}, u32[]{:S(2)}) %collective-permute-start.24) | collective-permute-done | bytes 196640 | tf_op jit(solution)/shard_map/ppermute | solution.py:361
  47.6 1.9 %collective-permute-start.16 = (bf16[256,256]{1,0:T(8,128)(2,1)S(1)}, bf16[256,256]{1,0:T(8,128)(2,1)S(1)}, u32[]{:S(2)}, u32[]{:S(2)}) collective-permute-start(bf16[256,256]{1,0:T(8,128)(2,1)S(1)} %shard_map.92.refs_2_), channel_id=1, source_target_pairs={{0,16},{4,20},{8,24},{12,28},{16,0},{20,4},{24,8},{28,12},{1,17},{... | collective-permute-start | bytes 393224 | tf_op jit(solution)/shard_map/ppermute | solution.py:361
  49.5 2.7 %collective-permute-done.22.refs_1_ = bf16[192,512]{1,0:T(8,128)(2,1)S(1)} collective-permute-done((bf16[192,512]{1,0:T(8,128)(2,1)S(1)}, bf16[192,512]{1,0:T(8,128)(2,1)S(1)}, u32[]{:S(2)}, u32[]{:S(2)}) %collective-permute-start.22) | collective-permute-done | bytes 196640 | tf_op jit(solution)/shard_map/ppermute | solution.py:361
  52.2 1.4 %collective-permute-start.17 = (bf16[256,256]{1,0:T(8,128)(2,1)S(1)}, bf16[256,256]{1,0:T(8,128)(2,1)S(1)}, u32[]{:S(2)}, u32[]{:S(2)}) collective-permute-start(bf16[256,256]{1,0:T(8,128)(2,1)S(1)} %shard_map.92.refs_2_), channel_id=1, source_target_pairs={{0,24},{4,28},{8,16},{12,20},{16,8},{20,12},{24,0},{28,4},{1,25},{... | collective-permute-start | bytes 393224 | tf_op jit(solution)/shard_map/ppermute | solution.py:361
  54.3 3.7 %collective-permute-start.26 = (bf16[192,128]{1,0:T(8,128)(2,1)S(1)}, bf16[192,128]{1,0:T(8,128)(2,1)S(1)}, u32[]{:S(2)}, u32[]{:S(2)}) collective-permute-start(bf16[192,128]{1,0:T(8,128)(2,1)S(1)} %get-tuple-element.64), channel_id=1, source_target_pairs={{0,2},{1,3},{2,0},{3,1},{4,6},{5,7},{6,4},{7,5},{8,10},{9,11},{10,... | collective-permute-start | bytes 147464 | tf_op jit(solution)/shard_map/ppermute | solution.py:358
  59.9 1.3 %collective-permute-start.19 = (bf16[208,128]{1,0:T(8,128)(2,1)S(1)}, bf16[208,128]{1,0:T(8,128)(2,1)S(1)}, u32[]{:S(2)}, u32[]{:S(2)}) collective-permute-start(bf16[208,128]{1,0:T(8,128)(2,1)S(1)} %get-tuple-element.53), channel_id=1, source_target_pairs={{0,1},{1,0},{2,3},{3,2},{4,7},{5,6},{6,5},{7,4},{8,9},{9,8},{10,11... | collective-permute-start | bytes 159752 | tf_op jit(solution)/shard_map/ppermute | solution.py:371
  62.4 1.6 %collective-permute-start.21 = (bf16[208,128]{1,0:T(8,128)(2,1)S(1)}, bf16[208,128]{1,0:T(8,128)(2,1)S(1)}, u32[]{:S(2)}, u32[]{:S(2)}) collective-permute-start(bf16[208,128]{1,0:T(8,128)(2,1)S(1)} %get-tuple-element.55), channel_id=1, source_target_pairs={{0,5},{1,4},{2,7},{3,6},{4,3},{5,2},{6,1},{7,0},{8,13},{9,12},{10,... | collective-permute-start | bytes 159752 | tf_op jit(solution)/shard_map/ppermute | solution.py:371
  68.1 1.3 %shard_map.94 = (bf16[192,2048]{1,0:T(8,128)(2,1)}, f32[1,2048]{1,0:T(1,128)}) custom-call(s32[4,4]{1,0:T(4,128)S(1)} %copy-done.1, bf16[192,2048]{1,0:T(8,128)(2,1)} %get-tuple-element.35.zero_ref, bf16[208,128]{1,0:T(8,128)(2,1)S(1)} %collective-permute-done.18.refs_0_, ...), custom_call_target="tpu_custom_call", output_to_operand_aliasing={{0}: (1, {})} | custom-call | flops 100000000 | bytes 1000000 | tf_op jit(solution)/shard_map/pallas_call | solution.py:39
  (48 shorter events, 15.0 us)
Async XLA Ops:
  2.9 17.2 %collective-permute-start.1 = (bf16[208,512]{1,0:T(8,128)(2,1)S(1)}, bf16[208,512]{1,0:T(8,128)(2,1)S(1)}, u32[]{:S(2)}, u32[]{:S(2)}) collective-permute-start(bf16[208,512]{1,0:T(8,128)(2,1)S(1)} %get-tuple-element.37), channel_id=1, source_target_pairs={{0,8},{4,12},{8,0},{12,4},{16,24},{20,28},{24,16},{28,20},{1,9},{5... | collective-permute-start | bytes 638984 | tf_op jit(solution)/shard_map/ppermute | solution.py:361
  7.5 10.4 %collective-permute-start.5 = (bf16[400,128]{1,0:T(8,128)(2,1)S(1)}, bf16[400,128]{1,0:T(8,128)(2,1)S(1)}, u32[]{:S(2)}, u32[]{:S(2)}) collective-permute-start(bf16[400,128]{1,0:T(8,128)(2,1)S(1)} %get-tuple-element.42), channel_id=1, source_target_pairs={{0,2},{1,3},{2,0},{3,1},{4,6},{5,7},{6,4},{7,5},{8,10},{9,11},{10,... | collective-permute-start | bytes 307208 | tf_op jit(solution)/shard_map/ppermute | solution.py:358
  10.1 7.8 %collective-permute-start.6 = (bf16[400,128]{1,0:T(8,128)(2,1)S(1)}, bf16[400,128]{1,0:T(8,128)(2,1)S(1)}, u32[]{:S(2)}, u32[]{:S(2)}) collective-permute-start(bf16[400,128]{1,0:T(8,128)(2,1)S(1)} %get-tuple-element.43), channel_id=1, source_target_pairs={{0,3},{1,2},{2,1},{3,0},{4,7},{5,6},{6,5},{7,4},{8,11},{9,10},{10,... | collective-permute-start | bytes 307208 | tf_op jit(solution)/shard_map/ppermute | solution.py:358
  10.3 13.7 %collective-permute-start.2 = (bf16[208,512]{1,0:T(8,128)(2,1)S(1)}, bf16[208,512]{1,0:T(8,128)(2,1)S(1)}, u32[]{:S(2)}, u32[]{:S(2)}) collective-permute-start(bf16[208,512]{1,0:T(8,128)(2,1)S(1)} %get-tuple-element.38), channel_id=1, source_target_pairs={{0,16},{4,20},{8,24},{12,28},{16,0},{20,4},{24,8},{28,12},{1,17},{... | collective-permute-start | bytes 638984 | tf_op jit(solution)/shard_map/ppermute | solution.py:361
  11.8 12.2 %collective-permute-start.3 = (bf16[208,512]{1,0:T(8,128)(2,1)S(1)}, bf16[208,512]{1,0:T(8,128)(2,1)S(1)}, u32[]{:S(2)}, u32[]{:S(2)}) collective-permute-start(bf16[208,512]{1,0:T(8,128)(2,1)S(1)} %get-tuple-element.39), channel_id=1, source_target_pairs={{0,24},{4,28},{8,16},{12,20},{16,8},{20,12},{24,0},{28,4},{1,25},{... | collective-permute-start | bytes 638984 | tf_op jit(solution)/shard_map/ppermute | solution.py:361
  18.0 6.0 %collective-permute-start.7 = (bf16[192,384]{1,0:T(8,128)(2,1)S(1)}, bf16[192,384]{1,0:T(8,128)(2,1)S(1)}, u32[]{:S(2)}, u32[]{:S(2)}) collective-permute-start(bf16[192,384]{1,0:T(8,128)(2,1)S(1)} %get-tuple-element.44.refs_4_), channel_id=1, source_target_pairs={{0,8},{4,12},{8,0},{12,4},{16,24},{20,28},{24,16},{28,20},{1,9},{5... | collective-permute-start | bytes 442376 | tf_op jit(solution)/shard_map/ppermute | solution.py:361
  18.6 8.6 %collective-permute-start.8 = (bf16[192,384]{1,0:T(8,128)(2,1)S(1)}, bf16[192,384]{1,0:T(8,128)(2,1)S(1)}, u32[]{:S(2)}, u32[]{:S(2)}) collective-permute-start(bf16[192,384]{1,0:T(8,128)(2,1)S(1)} %get-tuple-element.44.refs_4_), channel_id=1, source_target_pairs={{0,16},{4,20},{8,24},{12,28},{16,0},{20,4},{24,8},{28,12},{1,17},{... | collective-permute-start | bytes 442376 | tf_op jit(solution)/shard_map/ppermute | solution.py:361
  20.1 7.0 %collective-permute-start.9 = (bf16[192,384]{1,0:T(8,128)(2,1)S(1)}, bf16[192,384]{1,0:T(8,128)(2,1)S(1)}, u32[]{:S(2)}, u32[]{:S(2)}) collective-permute-start(bf16[192,384]{1,0:T(8,128)(2,1)S(1)} %get-tuple-element.44.refs_4_), channel_id=1, source_target_pairs={{0,24},{4,28},{8,16},{12,20},{16,8},{20,12},{24,0},{28,4},{1,25},{... | collective-permute-start | bytes 442376 | tf_op jit(solution)/shard_map/ppermute | solution.py:361
  27.7 6.8 %collective-permute-start.11 = (bf16[192,384]{1,0:T(8,128)(2,1)S(1)}, bf16[192,384]{1,0:T(8,128)(2,1)S(1)}, u32[]{:S(2)}, u32[]{:S(2)}) collective-permute-start(bf16[192,384]{1,0:T(8,128)(2,1)S(1)} %get-tuple-element.46.refs_4_), channel_id=1, source_target_pairs={{0,8},{4,12},{8,0},{12,4},{16,24},{20,28},{24,16},{28,20},{1,9},{5... | collective-permute-start | bytes 442376 | tf_op jit(solution)/shard_map/ppermute | solution.py:361
  28.3 8.1 %collective-permute-start.12 = (bf16[192,384]{1,0:T(8,128)(2,1)S(1)}, bf16[192,384]{1,0:T(8,128)(2,1)S(1)}, u32[]{:S(2)}, u32[]{:S(2)}) collective-permute-start(bf16[192,384]{1,0:T(8,128)(2,1)S(1)} %get-tuple-element.46.refs_4_), channel_id=1, source_target_pairs={{0,16},{4,20},{8,24},{12,28},{16,0},{20,4},{24,8},{28,12},{1,17},{... | collective-permute-start | bytes 442376 | tf_op jit(solution)/shard_map/ppermute | solution.py:361
  29.8 8.2 %collective-permute-start.13 = (bf16[192,384]{1,0:T(8,128)(2,1)S(1)}, bf16[192,384]{1,0:T(8,128)(2,1)S(1)}, u32[]{:S(2)}, u32[]{:S(2)}) collective-permute-start(bf16[192,384]{1,0:T(8,128)(2,1)S(1)} %get-tuple-element.46.refs_4_), channel_id=1, source_target_pairs={{0,24},{4,28},{8,16},{12,20},{16,8},{20,12},{24,0},{28,4},{1,25},{... | collective-permute-start | bytes 442376 | tf_op jit(solution)/shard_map/ppermute | solution.py:361
  31.3 23.0 %collective-permute-start = (bf16[192,1024]{1,0:T(8,128)(2,1)S(1)}, bf16[192,1024]{1,0:T(8,128)(2,1)S(1)}, u32[]{:S(2)}, u32[]{:S(2)}) collective-permute-start(bf16[192,1024]{1,0:T(8,128)(2,1)S(1)} %copy-done), channel_id=1, source_target_pairs={{0,4},{4,0},{8,12},{12,8},{16,20},{20,16},{24,28},{28,24},{1,5},{5... | collective-permute-start | bytes 1179656 | tf_op jit(solution)/shard_map/ppermute | solution.py:361
  38.8 8.8 %collective-permute-start.24 = (bf16[192,512]{1,0:T(8,128)(2,1)S(1)}, bf16[192,512]{1,0:T(8,128)(2,1)S(1)}, u32[]{:S(2)}, u32[]{:S(2)}) collective-permute-start(bf16[192,512]{1,0:T(8,128)(2,1)S(1)} %get-tuple-element.61), channel_id=1, source_target_pairs={{0,24},{4,28},{8,16},{12,20},{16,8},{20,12},{24,0},{28,4},{1,25},{... | collective-permute-start | bytes 589832 | tf_op jit(solution)/shard_map/ppermute | solution.py:361
  41.7 10.5 %collective-permute-start.22 = (bf16[192,512]{1,0:T(8,128)(2,1)S(1)}, bf16[192,512]{1,0:T(8,128)(2,1)S(1)}, u32[]{:S(2)}, u32[]{:S(2)}) collective-permute-start(bf16[192,512]{1,0:T(8,128)(2,1)S(1)} %get-tuple-element.59), channel_id=1, source_target_pairs={{0,8},{4,12},{8,0},{12,4},{16,24},{20,28},{24,16},{28,20},{1,9},{5... | collective-permute-start | bytes 589832 | tf_op jit(solution)/shard_map/ppermute | solution.py:361
  42.2 11.4 %collective-permute-start.23 = (bf16[192,512]{1,0:T(8,128)(2,1)S(1)}, bf16[192,512]{1,0:T(8,128)(2,1)S(1)}, u32[]{:S(2)}, u32[]{:S(2)}) collective-permute-start(bf16[192,512]{1,0:T(8,128)(2,1)S(1)} %get-tuple-element.60), channel_id=1, source_target_pairs={{0,16},{4,20},{8,24},{12,28},{16,0},{20,4},{24,8},{28,12},{1,17},{... | collective-permute-start | bytes 589832 | tf_op jit(solution)/shard_map/ppermute | solution.py:361
  42.4 15.5 %collective-permute-start.15 = (bf16[256,256]{1,0:T(8,128)(2,1)S(1)}, bf16[256,256]{1,0:T(8,128)(2,1)S(1)}, u32[]{:S(2)}, u32[]{:S(2)}) collective-permute-start(bf16[256,256]{1,0:T(8,128)(2,1)S(1)} %shard_map.92.refs_2_), channel_id=1, source_target_pairs={{0,8},{4,12},{8,0},{12,4},{16,24},{20,28},{24,16},{28,20},{1,9},{5... | collective-permute-start | bytes 393224 | tf_op jit(solution)/shard_map/ppermute | solution.py:361
  47.6 11.0 %collective-permute-start.16 = (bf16[256,256]{1,0:T(8,128)(2,1)S(1)}, bf16[256,256]{1,0:T(8,128)(2,1)S(1)}, u32[]{:S(2)}, u32[]{:S(2)}) collective-permute-start(bf16[256,256]{1,0:T(8,128)(2,1)S(1)} %shard_map.92.refs_2_), channel_id=1, source_target_pairs={{0,16},{4,20},{8,24},{12,28},{16,0},{20,4},{24,8},{28,12},{1,17},{... | collective-permute-start | bytes 393224 | tf_op jit(solution)/shard_map/ppermute | solution.py:361
  52.2 6.4 %collective-permute-start.17 = (bf16[256,256]{1,0:T(8,128)(2,1)S(1)}, bf16[256,256]{1,0:T(8,128)(2,1)S(1)}, u32[]{:S(2)}, u32[]{:S(2)}) collective-permute-start(bf16[256,256]{1,0:T(8,128)(2,1)S(1)} %shard_map.92.refs_2_), channel_id=1, source_target_pairs={{0,24},{4,28},{8,16},{12,20},{16,8},{20,12},{24,0},{28,4},{1,25},{... | collective-permute-start | bytes 393224 | tf_op jit(solution)/shard_map/ppermute | solution.py:361
  53.8 7.5 %collective-permute-start.25 = (bf16[192,128]{1,0:T(8,128)(2,1)S(1)}, bf16[192,128]{1,0:T(8,128)(2,1)S(1)}, u32[]{:S(2)}, u32[]{:S(2)}) collective-permute-start(bf16[192,128]{1,0:T(8,128)(2,1)S(1)} %get-tuple-element.63), channel_id=1, source_target_pairs={{0,1},{1,0},{2,3},{3,2},{4,5},{5,4},{6,7},{7,6},{8,9},{9,8},{10,11... | collective-permute-start | bytes 147464 | tf_op jit(solution)/shard_map/ppermute | solution.py:358
  54.3 8.2 %collective-permute-start.26 = (bf16[192,128]{1,0:T(8,128)(2,1)S(1)}, bf16[192,128]{1,0:T(8,128)(2,1)S(1)}, u32[]{:S(2)}, u32[]{:S(2)}) collective-permute-start(bf16[192,128]{1,0:T(8,128)(2,1)S(1)} %get-tuple-element.64), channel_id=1, source_target_pairs={{0,2},{1,3},{2,0},{3,1},{4,6},{5,7},{6,4},{7,5},{8,10},{9,11},{10,... | collective-permute-start | bytes 147464 | tf_op jit(solution)/shard_map/ppermute | solution.py:358
  57.9 7.4 %collective-permute-start.27 = (bf16[192,128]{1,0:T(8,128)(2,1)S(1)}, bf16[192,128]{1,0:T(8,128)(2,1)S(1)}, u32[]{:S(2)}, u32[]{:S(2)}) collective-permute-start(bf16[192,128]{1,0:T(8,128)(2,1)S(1)} %get-tuple-element.65), channel_id=1, source_target_pairs={{0,3},{1,2},{2,1},{3,0},{4,7},{5,6},{6,5},{7,4},{8,11},{9,10},{10,... | collective-permute-start | bytes 147464 | tf_op jit(solution)/shard_map/ppermute | solution.py:358
  59.3 8.0 %collective-permute-start.18 = (bf16[208,128]{1,0:T(8,128)(2,1)S(1)}, bf16[208,128]{1,0:T(8,128)(2,1)S(1)}, u32[]{:S(2)}, u32[]{:S(2)}) collective-permute-start(bf16[208,128]{1,0:T(8,128)(2,1)S(1)} %get-tuple-element.52), channel_id=1, source_target_pairs={{0,0},{1,1},{2,2},{3,3},{4,6},{5,7},{6,4},{7,5},{8,8},{9,9},{10,10... | collective-permute-start | bytes 159752 | tf_op jit(solution)/shard_map/ppermute | solution.py:371
  59.9 7.4 %collective-permute-start.19 = (bf16[208,128]{1,0:T(8,128)(2,1)S(1)}, bf16[208,128]{1,0:T(8,128)(2,1)S(1)}, u32[]{:S(2)}, u32[]{:S(2)}) collective-permute-start(bf16[208,128]{1,0:T(8,128)(2,1)S(1)} %get-tuple-element.53), channel_id=1, source_target_pairs={{0,1},{1,0},{2,3},{3,2},{4,7},{5,6},{6,5},{7,4},{8,9},{9,8},{10,11... | collective-permute-start | bytes 159752 | tf_op jit(solution)/shard_map/ppermute | solution.py:371
  61.3 6.1 %collective-permute-start.20 = (bf16[208,128]{1,0:T(8,128)(2,1)S(1)}, bf16[208,128]{1,0:T(8,128)(2,1)S(1)}, u32[]{:S(2)}, u32[]{:S(2)}) collective-permute-start(bf16[208,128]{1,0:T(8,128)(2,1)S(1)} %get-tuple-element.54), channel_id=1, source_target_pairs={{0,4},{1,5},{2,6},{3,7},{4,2},{5,3},{6,0},{7,1},{8,12},{9,13},{10,... | collective-permute-start | bytes 159752 | tf_op jit(solution)/shard_map/ppermute | solution.py:371
  (6 other events, 23.7 us)

commit v3 on v2

--- a/solution.py
+++ b/solution.py
@@ -10,7 +10,7 @@
 
 TILE = 128
 PARTS = 4
-EXTRA = 16
+EXTRA = 8
 F32 = jnp.float32
 BF16 = jnp.bfloat16
 
@@ -92,29 +92,45 @@
     return jnp.where(row == 0, line, live).astype(BF16)
 
 
-def pack_kernel(owners, tiles, parts, ids_ref, acts_ref, enc_ref, dec_ref, bias_ref, offset_ref, *rest):
-    moved, messages, bias_out, sem = rest[: owners - 1], rest[owners - 1 : -2], rest[-2], rest[-1]
+def pack_kernel(owners, tiles, parts, ids_in, acts_ref, enc_ref, dec_ref, bias_in, offset_in, *rest):
+    count = owners - 1
+    encs, decs, messages = rest[:count], rest[count : 2 * count], rest[2 * count : -6]
+    bias_out, ids_ref, bias_ref, offset_ref, small_sem, sem = rest[-6:]
+    small = []
+    for index, pair in enumerate(
+        ((ids_in, ids_ref), (bias_in, bias_ref), (offset_in, offset_ref))
+    ):
+        small.append(pltpu.make_async_copy(*pair, small_sem.at[index]))
+    for copy in small:
+        copy.start()
     features, rows = acts_ref.shape
     quarter = rows // parts
     me, part, _ = place(parts)
     inner = pl.ds(0, features)
+    early = []
+    for step in range(parts):
+        acts = acts_ref.at[:, lanes(xor(part, step), quarter)]
+        target = messages[step].at[inner, pl.ds(0, quarter)]
+        early.append(pltpu.make_async_copy(acts, target, small_sem.at[3 + step]))
+    for copy in early:
+        copy.start()
+    small[0].wait()
     pairs = []
     for step in range(1, owners):
         where = send_lanes(ids_ref, me, step, tiles)
-        for index, source in enumerate((enc_ref, dec_ref)):
-            target = moved[step - 1].at[pl.ds(index * features, features), :]
-            pairs.append((source.at[:, where], target))
+        pairs.append((enc_ref.at[:, where], encs[step - 1]))
+        pairs.append((dec_ref.at[:, where], decs[step - 1].at[inner, :]))
     here = send_lanes(ids_ref, me, 0, tiles)
     for step in range(parts):
-        acts = acts_ref.at[:, lanes(xor(part, step), quarter)]
-        start = 0
-        for source in (acts, enc_ref.at[:, here], dec_ref.at[:, here]):
-            size = source.shape[1]
-            pairs.append((source, messages[step].at[inner, pl.ds(start, size)]))
-            start += size
+        start = quarter
+        for source in (enc_ref.at[:, here], dec_ref.at[:, here]):
+            pairs.append((source, messages[step].at[inner, pl.ds(start, TILE)]))
+            start += TILE
     copies = [pltpu.make_async_copy(a, b, sem.at[i]) for i, (a, b) in enumerate(pairs)]
     for copy in copies:
         copy.start()
+    for copy in small[1:]:
+        copy.wait()
     offset = offset_ref[...]
     high = offset.astype(BF16)
     rest_one = offset - high.astype(F32)
@@ -128,20 +144,25 @@
         messages[step][pl.ds(features, EXTRA), :] = jnp.zeros((EXTRA, quarter + 2 * TILE), BF16)
         messages[step][pl.ds(features, EXTRA), pl.ds(0, features)] = split
     for step in range(1, owners):
-        moved[step - 1][pl.ds(2 * features, EXTRA), :] = bias_rows(ids_ref, bias_ref, me, step)
+        decs[step - 1][pl.ds(features, EXTRA), :] = bias_rows(ids_ref, bias_ref, me, step)
     bias_out[...] = bias_rows(ids_ref, bias_ref, me, 0)
-    for copy in copies:
+    for copy in early + copies:
         copy.wait()
 
 
-def join_kernel(owners, bias_ref, *refs):
-    got, enc_out, dec_out, bias_out = refs[: owners - 1], refs[-3], refs[-2], refs[-1]
-    features = enc_out.shape[0]
+def join_kernel(*refs):
+    out_ref = refs[-1]
+    for step, ref in enumerate(refs[:-1]):
+        out_ref[:, pl.ds(step * TILE, TILE)] = ref[...]
+
+
+def join_bias_kernel(owners, bias_ref, *refs):
+    got, out_ref, bias_out = refs[: owners - 1], refs[-2], refs[-1]
+    features = out_ref.shape[0]
     bias_out[:, pl.ds(0, TILE)] = bias_ref[...]
     for step in range(owners - 1):
-        enc_out[:, pl.ds(step * TILE, TILE)] = got[step][pl.ds(0, features), :]
-        dec_out[:, pl.ds(step * TILE, TILE)] = got[step][pl.ds(features, features), :]
-        bias_out[:, pl.ds((step + 1) * TILE, TILE)] = got[step][pl.ds(2 * features, EXTRA), :]
+        out_ref[:, pl.ds(step * TILE, TILE)] = got[step][pl.ds(0, features), :]
+        bias_out[:, pl.ds((step + 1) * TILE, TILE)] = got[step][pl.ds(features, EXTRA), :]
 
 
 def zero_kernel(*refs):
@@ -376,10 +397,11 @@
     bias_line = b_enc.reshape(tiles, TILE)
     packed = call(
         functools.partial(pack_kernel, owners, tiles, parts),
-        [shape(2 * features + EXTRA, TILE)] * (owners - 1)
+        [shape(features, TILE)] * (owners - 1)
+        + [shape(features + EXTRA, TILE)] * (owners - 1)
         + [shape(features + EXTRA, quarter + 2 * TILE)] * parts
         + [shape(EXTRA, TILE)],
-        [smem(), anywhere(), anywhere(), anywhere(), vmem(), vmem()],
+        [anywhere()] * 6,
         (
             in_hbm(tile_ids),
             in_hbm(activations),
@@ -388,17 +410,27 @@
             in_hbm(bias_line),
             in_hbm(b_dec.reshape(1, features)),
         ),
-        scratch=[pltpu.SemaphoreType.DMA((3 * parts + 2 * (owners - 1),))],
-    )
-    moved, messages, own_bias = packed[: owners - 1], packed[owners - 1 : -1], packed[-1]
-    moved = [over_lat(x, s + 1) for s, x in enumerate(moved)]
+        scratch=[
+            pltpu.SMEM(tile_ids.shape, jnp.int32),
+            pltpu.VMEM((tiles, TILE), BF16),
+            pltpu.VMEM((1, features), F32),
+            pltpu.SemaphoreType.DMA((3 + parts,)),
+            pltpu.SemaphoreType.DMA((2 * parts + 2 * (owners - 1),)),
+        ],
+    )
+    count = owners - 1
+    zenc, zdec = packed[:count], packed[count : 2 * count]
+    messages, own_bias = packed[2 * count : -1], packed[-1]
+    zenc = [over_lat(x, s + 1) for s, x in enumerate(zenc)]
+    zdec = [over_lat(x, s + 1) for s, x in enumerate(zdec)]
     messages = [messages[0]] + [over_layer(messages[s], s, cores) for s in range(1, parts)]
     all_acts = [activations] + [over_layer(activations, s, 1) for s in range(1, cores)]
-    enc_rest, dec_rest, bias_rows = call(
-        functools.partial(join_kernel, owners),
-        [shape(features, width - TILE)] * 2 + [shape(EXTRA, width)],
+    enc_rest = call(join_kernel, shape(features, width - TILE), [vmem()] * count, tuple(zenc))
+    dec_rest, bias_rows = call(
+        functools.partial(join_bias_kernel, owners),
+        [shape(features, width - TILE), shape(EXTRA, width)],
         [vmem()] * owners,
-        (own_bias, *moved),
+        (own_bias, *zdec),
     )
     encs = gather(enc_rest)
     decs = gather(dec_rest)
@@ -414,7 +446,7 @@
         mine = mine + over_layer(mine, step, 1)
         step = 2 * step
     other = over_layer(mine, step, 1)
-    groups = [[0], list(range(1, parts - 1)), [parts - 1]]
+    groups = [list(range(parts - 1)), [parts - 1]]
     total, sent = None, []
     for index, group in enumerate(groups):
         first, last = index == 0, index == len(groups) - 1
@@ -483,7 +515,7 @@
             functools.partial(place_kernel, owners, cores, tiles, parts, cross),
             outs,
             [smem(), anywhere()] + [vmem()] * owners,
-            (tile_ids, zero, *pieces),
+            (in_hbm(tile_ids), zero, *pieces),
             out_specs=[anywhere()] * len(outs),
             scratch=([pltpu.VMEM((1, latents), F32), pltpu.SemaphoreType.DMA] if cross else [])
             + [pltpu.VMEM((owners, features, TILE), BF16), pltpu.SemaphoreType.DMA((owners,))],

time: 69.7 us -> 82.1 us (1.18)
  waiting for transfers between devices: 22.2 us -> 34.8 us
    ppermute x18, waiting for transfers between devices: 16.5 us -> 23 us  [over_layer(): lax.ppermute(x, 'layer', [(i, i ^ step * stride) for i in range(layers)])]
    ppermute x6 -> x9, starting transfers between devices: 9.19 us -> 15.3 us  [over_lat(): return lax.ppermute(x, 'lat', [(i, i ^ step) for i in range(owners)])]
    ppermute x18, starting transfers between devices: 21.9 us -> 17.3 us  [over_layer(): lax.ppermute(x, 'layer', [(i, i ^ step * stride) for i in range(layers)])]
    ppermute x6 -> x9, waiting for transfers between devices: 4.86 us -> 9.27 us  [over_lat(): return lax.ppermute(x, 'lat', [(i, i ^ step) for i in range(owners)])]
    ppermute x4, waiting for transfers between devices: 0.84 us -> 2.44 us  [crossed(): return lax.ppermute(x, ('layer', 'lat'), pairs)]
    ppermute x4, starting transfers between devices: 4.71 us -> 3.74 us  [crossed(): return lax.ppermute(x, ('layer', 'lat'), pairs)]
  transfers between devices with their start and end apart: 28 -> 31, of which waited for: 10 -> 13; matrix products, arithmetic and copies ran while one was open for 0% -> 0% of each run, Pallas kernels for 9% -> 7%
where the time goes in v3:
time: 82.1 us; the launch traced here: 81.8 us
  starting transfers between devices  36.4 us (44%)
  waiting for transfers between devices  34.8 us (42%)
  Pallas kernels  9.85 us (12%)
    ppermute x18, waiting for transfers between devices, over_layer(): lax.ppermute(x, 'layer', [(i, i ^ step * stride) for i in range(layers)])  23 us
    ppermute x18, starting transfers between devices, over_layer(): lax.ppermute(x, 'layer', [(i, i ^ step * stride) for i in range(layers)])  17.3 us
    ppermute x9, starting transfers between devices, over_lat(): return lax.ppermute(x, 'lat', [(i, i ^ step) for i in range(owners)])  15.3 us
    pallas_call x12, Pallas kernels, call(): pl.pallas_call(kernel, out_shape=outs, in_specs=ins, out_specs=jax.tree.m...  9.85 us
    ppermute x9, waiting for transfers between devices, over_lat(): return lax.ppermute(x, 'lat', [(i, i ^ step) for i in range(owners)])  9.27 us
    ppermute x4, starting transfers between devices, crossed(): return lax.ppermute(x, ('layer', 'lat'), pairs)  3.74 us
    ppermute x4, waiting for transfers between devices, crossed(): return lax.ppermute(x, ('layer', 'lat'), pairs)  2.44 us
  transfers between devices with their start and end apart: 31, of which 13 were waited for; matrix products, arithmetic and copies ran while one was open for 0% of the time, Pallas kernels for 7%

profile of v3, /device:TPU:0, one launch (start us, length us, event | category | flops | bytes accessed | tf_op | source)
XLA Modules:
  0.0 81.8 jit_solution(4741716306161687065)
XLA Ops:
  0.6 2.1 %shard_map.86 = (bf16[192,128]{1,0:T(8,128)(2,1)S(1)}, bf16[192,128]{1,0:T(8,128)(2,1)S(1)}, bf16[192,128]{1,0:T(8,128)(2,1)S(1)}, bf16[200,128]{1,0:T(8,128)(2,...) custom-call(s32[4,4]{1,0:T(4,128)} %ids_ref.3, ...), custom_call_target="tpu_custom_call" | custom-call | flops 100000000 | bytes 1000000 | tf_op jit(solution)/shard_map/pallas_call | solution.py:39
  2.7 3.2 %collective-permute-start.4 = (bf16[192,128]{1,0:T(8,128)(2,1)S(1)}, bf16[192,128]{1,0:T(8,128)(2,1)S(1)}, u32[]{:S(2)}, u32[]{:S(2)}) collective-permute-start(bf16[192,128]{1,0:T(8,128)(2,1)S(1)} %get-tuple-element.41), channel_id=1, source_target_pairs={{0,1},{1,0},{2,3},{3,2},{4,5},{5,4},{6,7},{7,6},{8,9},{9,8},{10,11... | collective-permute-start | bytes 147464 | tf_op jit(solution)/shard_map/ppermute | solution.py:379
  5.9 2.7 %collective-permute-start.5 = (bf16[192,128]{1,0:T(8,128)(2,1)S(1)}, bf16[192,128]{1,0:T(8,128)(2,1)S(1)}, u32[]{:S(2)}, u32[]{:S(2)}) collective-permute-start(bf16[192,128]{1,0:T(8,128)(2,1)S(1)} %get-tuple-element.42), channel_id=1, source_target_pairs={{0,2},{1,3},{2,0},{3,1},{4,6},{5,7},{6,4},{7,5},{8,10},{9,11},{10,... | collective-permute-start | bytes 147464 | tf_op jit(solution)/shard_map/ppermute | solution.py:379
  8.5 3.2 %collective-permute-done.5.refs_1_ = bf16[192,128]{1,0:T(8,128)(2,1)S(1)} collective-permute-done((bf16[192,128]{1,0:T(8,128)(2,1)S(1)}, bf16[192,128]{1,0:T(8,128)(2,1)S(1)}, u32[]{:S(2)}, u32[]{:S(2)}) %collective-permute-start.5) | collective-permute-done | bytes 49184 | tf_op jit(solution)/shard_map/ppermute | solution.py:379
  11.8 2.6 %collective-permute-done.6.refs_2_ = bf16[192,128]{1,0:T(8,128)(2,1)S(1)} collective-permute-done((bf16[192,128]{1,0:T(8,128)(2,1)S(1)}, bf16[192,128]{1,0:T(8,128)(2,1)S(1)}, u32[]{:S(2)}, u32[]{:S(2)}) %collective-permute-start.6) | collective-permute-done | bytes 49184 | tf_op jit(solution)/shard_map/ppermute | solution.py:379
  14.5 1.6 %collective-permute-start.7 = (bf16[192,384]{1,0:T(8,128)(2,1)S(1)}, bf16[192,384]{1,0:T(8,128)(2,1)S(1)}, u32[]{:S(2)}, u32[]{:S(2)}) collective-permute-start(bf16[192,384]{1,0:T(8,128)(2,1)S(1)} %shard_map.87.refs_4_), channel_id=1, source_target_pairs={{0,8},{4,12},{8,0},{12,4},{16,24},{20,28},{24,16},{28,20},{1,9},{5... | collective-permute-start | bytes 442376 | tf_op jit(solution)/shard_map/ppermute | solution.py:382
  16.5 1.5 %collective-permute-start.2 = (bf16[200,512]{1,0:T(8,128)(2,1)S(1)}, bf16[200,512]{1,0:T(8,128)(2,1)S(1)}, u32[]{:S(2)}, u32[]{:S(2)}) collective-permute-start(bf16[200,512]{1,0:T(8,128)(2,1)S(1)} %get-tuple-element.39), channel_id=1, source_target_pairs={{0,16},{4,20},{8,24},{12,28},{16,0},{20,4},{24,8},{28,12},{1,17},{... | collective-permute-start | bytes 614408 | tf_op jit(solution)/shard_map/ppermute | solution.py:382
  19.5 1.5 %collective-permute-start.8 = (bf16[192,384]{1,0:T(8,128)(2,1)S(1)}, bf16[192,384]{1,0:T(8,128)(2,1)S(1)}, u32[]{:S(2)}, u32[]{:S(2)}) collective-permute-start(bf16[192,384]{1,0:T(8,128)(2,1)S(1)} %shard_map.87.refs_4_), channel_id=1, source_target_pairs={{0,16},{4,20},{8,24},{12,28},{16,0},{20,4},{24,8},{28,12},{1,17},{... | collective-permute-start | bytes 442376 | tf_op jit(solution)/shard_map/ppermute | solution.py:382
  21.2 2.4 %collective-permute-start.9 = (bf16[192,384]{1,0:T(8,128)(2,1)S(1)}, bf16[192,384]{1,0:T(8,128)(2,1)S(1)}, u32[]{:S(2)}, u32[]{:S(2)}) collective-permute-start(bf16[192,384]{1,0:T(8,128)(2,1)S(1)} %shard_map.87.refs_4_), channel_id=1, source_target_pairs={{0,24},{4,28},{8,16},{12,20},{16,8},{20,12},{24,0},{28,4},{1,25},{... | collective-permute-start | bytes 442376 | tf_op jit(solution)/shard_map/ppermute | solution.py:382
  23.7 8.4 %collective-permute-done.8.refs_6_ = bf16[192,384]{1,0:T(8,128)(2,1)S(1)} collective-permute-done((bf16[192,384]{1,0:T(8,128)(2,1)S(1)}, bf16[192,384]{1,0:T(8,128)(2,1)S(1)}, u32[]{:S(2)}, u32[]{:S(2)}) %collective-permute-start.8) | collective-permute-done | bytes 147488 | tf_op jit(solution)/shard_map/ppermute | solution.py:382
  34.1 3.0 %collective-permute-start.13 = (bf16[200,128]{1,0:T(8,128)(2,1)S(1)}, bf16[200,128]{1,0:T(8,128)(2,1)S(1)}, u32[]{:S(2)}, u32[]{:S(2)}) collective-permute-start(bf16[200,128]{1,0:T(8,128)(2,1)S(1)} %get-tuple-element.47), channel_id=1, source_target_pairs={{0,3},{1,2},{2,1},{3,0},{4,7},{5,6},{6,5},{7,4},{8,11},{9,10},{10,... | collective-permute-start | bytes 153608 | tf_op jit(solution)/shard_map/ppermute | solution.py:379
  37.6 3.0 %collective-permute-done.12.refs_1_ = bf16[200,128]{1,0:T(8,128)(2,1)S(1)} collective-permute-done((bf16[200,128]{1,0:T(8,128)(2,1)S(1)}, bf16[200,128]{1,0:T(8,128)(2,1)S(1)}, u32[]{:S(2)}, u32[]{:S(2)}) %collective-permute-start.12) | collective-permute-done | bytes 51232 | tf_op jit(solution)/shard_map/ppermute | solution.py:379
  41.9 1.5 %collective-permute-start.15 = (bf16[192,384]{1,0:T(8,128)(2,1)S(1)}, bf16[192,384]{1,0:T(8,128)(2,1)S(1)}, u32[]{:S(2)}, u32[]{:S(2)}) collective-permute-start(bf16[192,384]{1,0:T(8,128)(2,1)S(1)} %get-tuple-element.49.refs_6_), channel_id=1, source_target_pairs={{0,16},{4,20},{8,24},{12,28},{16,0},{20,4},{24,8},{28,12},{1,17},{... | collective-permute-start | bytes 442376 | tf_op jit(solution)/shard_map/ppermute | solution.py:382
  44.1 3.1 %collective-permute-done.14.refs_7_ = bf16[192,384]{1,0:T(8,128)(2,1)S(1)} collective-permute-done((bf16[192,384]{1,0:T(8,128)(2,1)S(1)}, bf16[192,384]{1,0:T(8,128)(2,1)S(1)}, u32[]{:S(2)}, u32[]{:S(2)}) %collective-permute-start.14) | collective-permute-done | bytes 147488 | tf_op jit(solution)/shard_map/ppermute | solution.py:382
  47.2 2.7 %collective-permute-done.15.refs_8_ = bf16[192,384]{1,0:T(8,128)(2,1)S(1)} collective-permute-done((bf16[192,384]{1,0:T(8,128)(2,1)S(1)}, bf16[192,384]{1,0:T(8,128)(2,1)S(1)}, u32[]{:S(2)}, u32[]{:S(2)}) %collective-permute-start.15) | collective-permute-done | bytes 147488 | tf_op jit(solution)/shard_map/ppermute | solution.py:382
  49.9 1.6 %shard_map.90 = (bf16[512,256]{1,0:T(8,128)(2,1)S(1)}, bf16[192,512]{1,0:T(8,128)(2,1)S(1)}, bf16[192,512]{1,0:T(8,128)(2,1)S(1)}, bf16[192,512]{1,0:T(8,128)(2,1)S(1)}, f32[512,256]{1,0:T(8,128)S(1)}) custom-call(f32[512,256]{1,0:T(8,128)S(1)} %shard_map.88.refs_0_, f32[512,256]{1,0:T(8,128)S(1)} %collective-permute-done.10.refs_1_, ...), custom_call_target="tpu_custom_call" | custom-call | flops 100000000 | bytes 1000000 | tf_op jit(solution)/shard_map/pallas_call | solution.py:39
  53.3 1.5 %collective-permute-start.25 = (bf16[192,512]{1,0:T(8,128)(2,1)S(1)}, bf16[192,512]{1,0:T(8,128)(2,1)S(1)}, u32[]{:S(2)}, u32[]{:S(2)}) collective-permute-start(bf16[192,512]{1,0:T(8,128)(2,1)S(1)} %get-tuple-element.61), channel_id=1, source_target_pairs={{0,8},{4,12},{8,0},{12,4},{16,24},{20,28},{24,16},{28,20},{1,9},{5... | collective-permute-start | bytes 589832 | tf_op jit(solution)/shard_map/ppermute | solution.py:382
  56.0 5.1 %collective-permute-done.27.refs_3_ = bf16[192,512]{1,0:T(8,128)(2,1)S(1)} collective-permute-done((bf16[192,512]{1,0:T(8,128)(2,1)S(1)}, bf16[192,512]{1,0:T(8,128)(2,1)S(1)}, u32[]{:S(2)}, u32[]{:S(2)}) %collective-permute-start.27) | collective-permute-done | bytes 196640 | tf_op jit(solution)/shard_map/ppermute | solution.py:382
  62.1 2.7 %collective-permute-done.25.refs_1_ = bf16[192,512]{1,0:T(8,128)(2,1)S(1)} collective-permute-done((bf16[192,512]{1,0:T(8,128)(2,1)S(1)}, bf16[192,512]{1,0:T(8,128)(2,1)S(1)}, u32[]{:S(2)}, u32[]{:S(2)}) %collective-permute-start.25) | collective-permute-done | bytes 196640 | tf_op jit(solution)/shard_map/ppermute | solution.py:382
  64.9 1.5 %collective-permute-start.28 = (bf16[192,128]{1,0:T(8,128)(2,1)S(1)}, bf16[192,128]{1,0:T(8,128)(2,1)S(1)}, u32[]{:S(2)}, u32[]{:S(2)}) collective-permute-start(bf16[192,128]{1,0:T(8,128)(2,1)S(1)} %get-tuple-element.65), channel_id=1, source_target_pairs={{0,1},{1,0},{2,3},{3,2},{4,5},{5,4},{6,7},{7,6},{8,9},{9,8},{10,11... | collective-permute-start | bytes 147464 | tf_op jit(solution)/shard_map/ppermute | solution.py:379
  66.5 1.7 %collective-permute-start.29 = (bf16[192,128]{1,0:T(8,128)(2,1)S(1)}, bf16[192,128]{1,0:T(8,128)(2,1)S(1)}, u32[]{:S(2)}, u32[]{:S(2)}) collective-permute-start(bf16[192,128]{1,0:T(8,128)(2,1)S(1)} %get-tuple-element.66), channel_id=1, source_target_pairs={{0,2},{1,3},{2,0},{3,1},{4,6},{5,7},{6,4},{7,5},{8,10},{9,11},{10,... | collective-permute-start | bytes 147464 | tf_op jit(solution)/shard_map/ppermute | solution.py:379
  68.2 1.7 %collective-permute-start.30 = (bf16[192,128]{1,0:T(8,128)(2,1)S(1)}, bf16[192,128]{1,0:T(8,128)(2,1)S(1)}, u32[]{:S(2)}, u32[]{:S(2)}) collective-permute-start(bf16[192,128]{1,0:T(8,128)(2,1)S(1)} %get-tuple-element.67), channel_id=1, source_target_pairs={{0,3},{1,2},{2,1},{3,0},{4,7},{5,6},{6,5},{7,4},{8,11},{9,10},{10,... | collective-permute-start | bytes 147464 | tf_op jit(solution)/shard_map/ppermute | solution.py:379
  72.1 1.5 %collective-permute-start.22 = (bf16[200,128]{1,0:T(8,128)(2,1)S(1)}, bf16[200,128]{1,0:T(8,128)(2,1)S(1)}, u32[]{:S(2)}, u32[]{:S(2)}) collective-permute-start(bf16[200,128]{1,0:T(8,128)(2,1)S(1)} %get-tuple-element.55), channel_id=1, source_target_pairs={{0,1},{1,0},{2,3},{3,2},{4,7},{5,6},{6,5},{7,4},{8,9},{9,8},{10,11... | collective-permute-start | bytes 153608 | tf_op jit(solution)/shard_map/ppermute | solution.py:392
  78.6 1.7 %collective-permute-done.24.refs_3_ = bf16[200,128]{1,0:T(8,128)(2,1)S(1)} collective-permute-done((bf16[200,128]{1,0:T(8,128)(2,1)S(1)}, bf16[200,128]{1,0:T(8,128)(2,1)S(1)}, u32[]{:S(2)}, u32[]{:S(2)}) %collective-permute-start.24) | collective-permute-done | bytes 51232 | tf_op jit(solution)/shard_map/ppermute | solution.py:392
  (52 shorter events, 19.2 us)
Async XLA Ops:
  5.9 5.9 %collective-permute-start.5 = (bf16[192,128]{1,0:T(8,128)(2,1)S(1)}, bf16[192,128]{1,0:T(8,128)(2,1)S(1)}, u32[]{:S(2)}, u32[]{:S(2)}) collective-permute-start(bf16[192,128]{1,0:T(8,128)(2,1)S(1)} %get-tuple-element.42), channel_id=1, source_target_pairs={{0,2},{1,3},{2,0},{3,1},{4,6},{5,7},{6,4},{7,5},{8,10},{9,11},{10,... | collective-permute-start | bytes 147464 | tf_op jit(solution)/shard_map/ppermute | solution.py:379
  8.5 5.9 %collective-permute-start.6 = (bf16[192,128]{1,0:T(8,128)(2,1)S(1)}, bf16[192,128]{1,0:T(8,128)(2,1)S(1)}, u32[]{:S(2)}, u32[]{:S(2)}) collective-permute-start(bf16[192,128]{1,0:T(8,128)(2,1)S(1)} %get-tuple-element.43), channel_id=1, source_target_pairs={{0,3},{1,2},{2,1},{3,0},{4,7},{5,6},{6,5},{7,4},{8,11},{9,10},{10,... | collective-permute-start | bytes 147464 | tf_op jit(solution)/shard_map/ppermute | solution.py:379
  14.5 6.8 %collective-permute-start.7 = (bf16[192,384]{1,0:T(8,128)(2,1)S(1)}, bf16[192,384]{1,0:T(8,128)(2,1)S(1)}, u32[]{:S(2)}, u32[]{:S(2)}) collective-permute-start(bf16[192,384]{1,0:T(8,128)(2,1)S(1)} %shard_map.87.refs_4_), channel_id=1, source_target_pairs={{0,8},{4,12},{8,0},{12,4},{16,24},{20,28},{24,16},{28,20},{1,9},{5... | collective-permute-start | bytes 442376 | tf_op jit(solution)/shard_map/ppermute | solution.py:382
  16.0 16.1 %collective-permute-start.1 = (bf16[200,512]{1,0:T(8,128)(2,1)S(1)}, bf16[200,512]{1,0:T(8,128)(2,1)S(1)}, u32[]{:S(2)}, u32[]{:S(2)}) collective-permute-start(bf16[200,512]{1,0:T(8,128)(2,1)S(1)} %get-tuple-element.38), channel_id=1, source_target_pairs={{0,8},{4,12},{8,0},{12,4},{16,24},{20,28},{24,16},{28,20},{1,9},{5... | collective-permute-start | bytes 614408 | tf_op jit(solution)/shard_map/ppermute | solution.py:382
  16.5 15.6 %collective-permute-start.2 = (bf16[200,512]{1,0:T(8,128)(2,1)S(1)}, bf16[200,512]{1,0:T(8,128)(2,1)S(1)}, u32[]{:S(2)}, u32[]{:S(2)}) collective-permute-start(bf16[200,512]{1,0:T(8,128)(2,1)S(1)} %get-tuple-element.39), channel_id=1, source_target_pairs={{0,16},{4,20},{8,24},{12,28},{16,0},{20,4},{24,8},{28,12},{1,17},{... | collective-permute-start | bytes 614408 | tf_op jit(solution)/shard_map/ppermute | solution.py:382
  18.1 14.1 %collective-permute-start.3 = (bf16[200,512]{1,0:T(8,128)(2,1)S(1)}, bf16[200,512]{1,0:T(8,128)(2,1)S(1)}, u32[]{:S(2)}, u32[]{:S(2)}) collective-permute-start(bf16[200,512]{1,0:T(8,128)(2,1)S(1)} %get-tuple-element.40), channel_id=1, source_target_pairs={{0,24},{4,28},{8,16},{12,20},{16,8},{20,12},{24,0},{28,4},{1,25},{... | collective-permute-start | bytes 614408 | tf_op jit(solution)/shard_map/ppermute | solution.py:382
  19.5 12.6 %collective-permute-start.8 = (bf16[192,384]{1,0:T(8,128)(2,1)S(1)}, bf16[192,384]{1,0:T(8,128)(2,1)S(1)}, u32[]{:S(2)}, u32[]{:S(2)}) collective-permute-start(bf16[192,384]{1,0:T(8,128)(2,1)S(1)} %shard_map.87.refs_4_), channel_id=1, source_target_pairs={{0,16},{4,20},{8,24},{12,28},{16,0},{20,4},{24,8},{28,12},{1,17},{... | collective-permute-start | bytes 442376 | tf_op jit(solution)/shard_map/ppermute | solution.py:382
  21.2 10.9 %collective-permute-start.9 = (bf16[192,384]{1,0:T(8,128)(2,1)S(1)}, bf16[192,384]{1,0:T(8,128)(2,1)S(1)}, u32[]{:S(2)}, u32[]{:S(2)}) collective-permute-start(bf16[192,384]{1,0:T(8,128)(2,1)S(1)} %shard_map.87.refs_4_), channel_id=1, source_target_pairs={{0,24},{4,28},{8,16},{12,20},{16,8},{20,12},{24,0},{28,4},{1,25},{... | collective-permute-start | bytes 442376 | tf_op jit(solution)/shard_map/ppermute | solution.py:382
  32.6 17.3 %collective-permute-start.10 = (f32[512,256]{1,0:T(8,128)S(1)}, f32[512,256]{1,0:T(8,128)S(1)}, u32[]{:S(2)}, u32[]{:S(2)}) collective-permute-start(f32[512,256]{1,0:T(8,128)S(1)} %shard_map.88.refs_0_), channel_id=1, source_target_pairs={{0,4},{4,0},{8,12},{12,8},{16,20},{20,16},{24,28},{28,24},{1,5},{5... | collective-permute-start | bytes 1572872 | tf_op jit(solution)/shard_map/ppermute | solution.py:382
  32.8 7.8 %collective-permute-start.12 = (bf16[200,128]{1,0:T(8,128)(2,1)S(1)}, bf16[200,128]{1,0:T(8,128)(2,1)S(1)}, u32[]{:S(2)}, u32[]{:S(2)}) collective-permute-start(bf16[200,128]{1,0:T(8,128)(2,1)S(1)} %get-tuple-element.46), channel_id=1, source_target_pairs={{0,2},{1,3},{2,0},{3,1},{4,6},{5,7},{6,4},{7,5},{8,10},{9,11},{10,... | collective-permute-start | bytes 153608 | tf_op jit(solution)/shard_map/ppermute | solution.py:379
  34.1 6.4 %collective-permute-start.13 = (bf16[200,128]{1,0:T(8,128)(2,1)S(1)}, bf16[200,128]{1,0:T(8,128)(2,1)S(1)}, u32[]{:S(2)}, u32[]{:S(2)}) collective-permute-start(bf16[200,128]{1,0:T(8,128)(2,1)S(1)} %get-tuple-element.47), channel_id=1, source_target_pairs={{0,3},{1,2},{2,1},{3,0},{4,7},{5,6},{6,5},{7,4},{8,11},{9,10},{10,... | collective-permute-start | bytes 153608 | tf_op jit(solution)/shard_map/ppermute | solution.py:379
  40.6 6.6 %collective-permute-start.14 = (bf16[192,384]{1,0:T(8,128)(2,1)S(1)}, bf16[192,384]{1,0:T(8,128)(2,1)S(1)}, u32[]{:S(2)}, u32[]{:S(2)}) collective-permute-start(bf16[192,384]{1,0:T(8,128)(2,1)S(1)} %get-tuple-element.49.refs_6_), channel_id=1, source_target_pairs={{0,8},{4,12},{8,0},{12,4},{16,24},{20,28},{24,16},{28,20},{1,9},{5... | collective-permute-start | bytes 442376 | tf_op jit(solution)/shard_map/ppermute | solution.py:382
  41.9 8.0 %collective-permute-start.15 = (bf16[192,384]{1,0:T(8,128)(2,1)S(1)}, bf16[192,384]{1,0:T(8,128)(2,1)S(1)}, u32[]{:S(2)}, u32[]{:S(2)}) collective-permute-start(bf16[192,384]{1,0:T(8,128)(2,1)S(1)} %get-tuple-element.49.refs_6_), channel_id=1, source_target_pairs={{0,16},{4,20},{8,24},{12,28},{16,0},{20,4},{24,8},{28,12},{1,17},{... | collective-permute-start | bytes 442376 | tf_op jit(solution)/shard_map/ppermute | solution.py:382
  43.5 8.1 %collective-permute-start.16 = (bf16[192,384]{1,0:T(8,128)(2,1)S(1)}, bf16[192,384]{1,0:T(8,128)(2,1)S(1)}, u32[]{:S(2)}, u32[]{:S(2)}) collective-permute-start(bf16[192,384]{1,0:T(8,128)(2,1)S(1)} %get-tuple-element.49.refs_6_), channel_id=1, source_target_pairs={{0,24},{4,28},{8,16},{12,20},{16,8},{20,12},{24,0},{28,4},{1,25},{... | collective-permute-start | bytes 442376 | tf_op jit(solution)/shard_map/ppermute | solution.py:382
  44.1 22.3 %collective-permute-start = (bf16[192,1024]{1,0:T(8,128)(2,1)S(1)}, bf16[192,1024]{1,0:T(8,128)(2,1)S(1)}, u32[]{:S(2)}, u32[]{:S(2)}) collective-permute-start(bf16[192,1024]{1,0:T(8,128)(2,1)S(1)} %copy-done), channel_id=1, source_target_pairs={{0,4},{4,0},{8,12},{12,8},{16,20},{20,16},{24,28},{28,24},{1,5},{5... | collective-permute-start | bytes 1179656 | tf_op jit(solution)/shard_map/ppermute | solution.py:382
  52.3 8.8 %collective-permute-start.27 = (bf16[192,512]{1,0:T(8,128)(2,1)S(1)}, bf16[192,512]{1,0:T(8,128)(2,1)S(1)}, u32[]{:S(2)}, u32[]{:S(2)}) collective-permute-start(bf16[192,512]{1,0:T(8,128)(2,1)S(1)} %get-tuple-element.63), channel_id=1, source_target_pairs={{0,24},{4,28},{8,16},{12,20},{16,8},{20,12},{24,0},{28,4},{1,25},{... | collective-permute-start | bytes 589832 | tf_op jit(solution)/shard_map/ppermute | solution.py:382
  53.3 11.5 %collective-permute-start.25 = (bf16[192,512]{1,0:T(8,128)(2,1)S(1)}, bf16[192,512]{1,0:T(8,128)(2,1)S(1)}, u32[]{:S(2)}, u32[]{:S(2)}) collective-permute-start(bf16[192,512]{1,0:T(8,128)(2,1)S(1)} %get-tuple-element.61), channel_id=1, source_target_pairs={{0,8},{4,12},{8,0},{12,4},{16,24},{20,28},{24,16},{28,20},{1,9},{5... | collective-permute-start | bytes 589832 | tf_op jit(solution)/shard_map/ppermute | solution.py:382
  54.8 10.0 %collective-permute-start.26 = (bf16[192,512]{1,0:T(8,128)(2,1)S(1)}, bf16[192,512]{1,0:T(8,128)(2,1)S(1)}, u32[]{:S(2)}, u32[]{:S(2)}) collective-permute-start(bf16[192,512]{1,0:T(8,128)(2,1)S(1)} %get-tuple-element.62), channel_id=1, source_target_pairs={{0,16},{4,20},{8,24},{12,28},{16,0},{20,4},{24,8},{28,12},{1,17},{... | collective-permute-start | bytes 589832 | tf_op jit(solution)/shard_map/ppermute | solution.py:382
  55.9 12.3 %collective-permute-start.18 = (bf16[256,256]{1,0:T(8,128)(2,1)S(1)}, bf16[256,256]{1,0:T(8,128)(2,1)S(1)}, u32[]{:S(2)}, u32[]{:S(2)}) collective-permute-start(bf16[256,256]{1,0:T(8,128)(2,1)S(1)} %shard_map.92.refs_2_), channel_id=1, source_target_pairs={{0,8},{4,12},{8,0},{12,4},{16,24},{20,28},{24,16},{28,20},{1,9},{5... | collective-permute-start | bytes 393224 | tf_op jit(solution)/shard_map/ppermute | solution.py:382
  61.0 8.9 %collective-permute-start.19 = (bf16[256,256]{1,0:T(8,128)(2,1)S(1)}, bf16[256,256]{1,0:T(8,128)(2,1)S(1)}, u32[]{:S(2)}, u32[]{:S(2)}) collective-permute-start(bf16[256,256]{1,0:T(8,128)(2,1)S(1)} %shard_map.92.refs_2_), channel_id=1, source_target_pairs={{0,16},{4,20},{8,24},{12,28},{16,0},{20,4},{24,8},{28,12},{1,17},{... | collective-permute-start | bytes 393224 | tf_op jit(solution)/shard_map/ppermute | solution.py:382
  64.9 8.7 %collective-permute-start.28 = (bf16[192,128]{1,0:T(8,128)(2,1)S(1)}, bf16[192,128]{1,0:T(8,128)(2,1)S(1)}, u32[]{:S(2)}, u32[]{:S(2)}) collective-permute-start(bf16[192,128]{1,0:T(8,128)(2,1)S(1)} %get-tuple-element.65), channel_id=1, source_target_pairs={{0,1},{1,0},{2,3},{3,2},{4,5},{5,4},{6,7},{7,6},{8,9},{9,8},{10,11... | collective-permute-start | bytes 147464 | tf_op jit(solution)/shard_map/ppermute | solution.py:379
  66.5 8.2 %collective-permute-start.29 = (bf16[192,128]{1,0:T(8,128)(2,1)S(1)}, bf16[192,128]{1,0:T(8,128)(2,1)S(1)}, u32[]{:S(2)}, u32[]{:S(2)}) collective-permute-start(bf16[192,128]{1,0:T(8,128)(2,1)S(1)} %get-tuple-element.66), channel_id=1, source_target_pairs={{0,2},{1,3},{2,0},{3,1},{4,6},{5,7},{6,4},{7,5},{8,10},{9,11},{10,... | collective-permute-start | bytes 147464 | tf_op jit(solution)/shard_map/ppermute | solution.py:379
  68.2 8.2 %collective-permute-start.30 = (bf16[192,128]{1,0:T(8,128)(2,1)S(1)}, bf16[192,128]{1,0:T(8,128)(2,1)S(1)}, u32[]{:S(2)}, u32[]{:S(2)}) collective-permute-start(bf16[192,128]{1,0:T(8,128)(2,1)S(1)} %get-tuple-element.67), channel_id=1, source_target_pairs={{0,3},{1,2},{2,1},{3,0},{4,7},{5,6},{6,5},{7,4},{8,11},{9,10},{10,... | collective-permute-start | bytes 147464 | tf_op jit(solution)/shard_map/ppermute | solution.py:379
  71.4 6.5 %collective-permute-start.21 = (bf16[200,128]{1,0:T(8,128)(2,1)S(1)}, bf16[200,128]{1,0:T(8,128)(2,1)S(1)}, u32[]{:S(2)}, u32[]{:S(2)}) collective-permute-start(bf16[200,128]{1,0:T(8,128)(2,1)S(1)} %get-tuple-element.54), channel_id=1, source_target_pairs={{0,0},{1,1},{2,2},{3,3},{4,6},{5,7},{6,4},{7,5},{8,8},{9,9},{10,10... | collective-permute-start | bytes 153608 | tf_op jit(solution)/shard_map/ppermute | solution.py:392
  (8 other events, 48.7 us)
